TPU v7x, 256 devices: a whole 4x4x8 slice. The times are simulated.
256 devices in a mesh: seq: 32 (over x_lo, z, core), chan: 8 (over x_hi, y).
Axes of the slice: x: 4 (x_hi: 2, x_lo: 2; x = x_hi * 2 + x_lo), y: 4, z: 8, core: 2. Of those that a mesh axis runs over, the one named last changes fastest.
Arguments:
- inputs: bfloat16 [262144, 1024], P('seq', 'chan'), may hold values from -6 to 6
- out_grad: bfloat16 [262144, 1024], P('seq', 'chan'), may hold values from -6 to 6
- kernel: bfloat16 [512, 512, 1024], P('seq', None, 'chan'), may hold values from -4 to 4
- gate_weight: bfloat16 [1024, 1024], P(None, 'chan'), may hold values from -0.1875 to 0.1875
- right_factor: bfloat16 [512, 512], replicated, may hold values from -0.25 to 0.25
- left_factor: bfloat16 [512, 512], replicated, may hold values from -0.25 to 0.25
Outputs:
- input_grad: bfloat16 [262144, 1024], P('seq', 'chan')
- kernel_grad: bfloat16 [512, 512, 1024], P('seq', None, 'chan')
- right_grad: float32 [262144], P(('seq', 'chan'))
- left_grad: float32 [262144], P(('seq', 'chan'))
- gate_weight_grad: float32 [1024, 1024], P(('seq', 'chan'))
All inputs are finite; a program needn't handle non-finite values.
Results may differ from a plain program's by a relative error of at most 0.015.
Values may be sent and summed in bfloat16 or wider, within the bound.
No kernel may reach another device: no remote copies, remote signals or barrier semaphores. Data moves between devices by JAX's collectives and lax.ppermute only.
A program may use at most 128 MiB of HBM per device.

v0:
```python
import functools

import jax
import jax.numpy as jnp
from jax import lax
from jax.experimental import pallas as pl
from jax.experimental.pallas import tpu as pltpu
from jax.sharding import PartitionSpec as P


F32 = jnp.float32
BF16 = jnp.bfloat16
NT = (((1,), (1,)), ((), ()))


def call(body, grid, in_specs, out_specs, out_shape, scratch, flops, nbytes):
    return pl.pallas_call(
        body,
        grid_spec=pltpu.PrefetchScalarGridSpec(
            num_scalar_prefetch=1,
            grid=grid,
            in_specs=in_specs,
            out_specs=out_specs,
            scratch_shapes=scratch,
        ),
        out_shape=out_shape,
        cost_estimate=pl.CostEstimate(flops=flops, bytes_accessed=nbytes, transcendentals=0),
        compiler_params=pltpu.CompilerParams(vmem_limit_bytes=48 * 2**20),
    )


def lanes(parts):
    return jnp.concatenate(parts, axis=1)


def first_body(me, x_ref, k_ref, r_ref, u_ref, v_ref, scr, *, step):
    g = pl.program_id(0)
    heads, block = scr.shape[0] // r_ref.shape[0], r_ref.shape[0]
    rhs = lanes([x_ref[t] for t in range(step)])
    prod = jnp.dot(r_ref[...], rhs, preferred_element_type=F32).astype(BF16)
    for t in range(step):
        u = prod[:, t * 128 : (t + 1) * 128]
        u_ref[t] = u
        v = (u.astype(F32) * k_ref[t].astype(F32)).astype(BF16)
        scr[pl.ds(g * step + t, block, stride=heads), :] = v.astype(F32)

    @pl.when(g == pl.num_programs(0) - 1)
    def _():
        def put(s, carry):
            rows = scr[pl.ds(pl.multiple_of(s * heads * heads, 256), heads * heads), :]
            v_ref[s] = rows.reshape(heads, heads, 128).astype(BF16)
            return carry

        lax.fori_loop(0, v_ref.shape[0], put, 0)


def mix_body(me, p_ref, og_ref, l_ref, *outs):
    t = pl.program_id(0)
    block = l_ref.shape[0]
    rhs = lanes([p_ref[:, u].reshape(block, 128) for u in range(2)])
    mixed = jnp.dot(l_ref[...], rhs, preferred_element_type=F32).astype(BF16).astype(F32)
    both = jnp.concatenate(
        [(og_ref[u].astype(F32) * mixed[:, u * 128 : (u + 1) * 128]).astype(BF16) for u in range(2)],
        axis=0,
    )
    for q in range(len(outs)):

        @pl.when(t == q)
        def _(q=q):
            outs[q][...] = both


def gate_body(me, x_ref, *refs, n):
    quads, gs, wcat, scr = refs[:4], refs[4 : 4 + n], refs[4 + n], refs[5 + n]

    @pl.when(pl.program_id(0) == 0)
    def _():
        quarter = scr.shape[0] // 4
        ways = quads[0].shape[0]
        for k in range(4):
            spot = (me[1] ^ (k // 2)) * 2 + (me[2] ^ (k % 2))
            rows = pl.ds(pl.multiple_of(spot * quarter, quarter), quarter)
            for q in range(n):
                scr[rows, q * 128 : (q + 1) * 128] = quads[k][q % ways, q // ways]
        wcat[...] = scr[...]

    rows_in = lanes([x_ref[r] for r in range(n)])
    pre = jnp.dot(rows_in, scr[...], preferred_element_type=F32)
    gate = jax.nn.sigmoid(pre).astype(BF16)
    for q in range(n):
        gs[q][...] = gate[:, q * 128 : (q + 1) * 128]


def turn_body(me, x_ref, out, *, n, seqs):
    g = pl.program_id(0)
    rows, width = out.shape[0], n * 128
    rho = lax.broadcasted_iota(jnp.int32, (rows, width), 0) + g * rows
    col = lax.broadcasted_iota(jnp.int32, (rows, width), 1)
    per = width // (2 * n)
    high = seqs // 2
    own = per // high
    core = me[1] ^ (rho // (width // 2))
    rest = lax.rem(rho, width // 2)
    inner = lax.rem(rest, per)
    seq = lax.rem(inner, high) * 2 + core
    want = (seq * n + (me[0] ^ (rest // per))) * own + inner // high
    pick = jnp.where(want == col, 1.0, 0.0).astype(BF16)
    rows_in = lanes([x_ref[r] for r in range(n)])
    out[...] = lax.dot_general(pick, rows_in, NT, preferred_element_type=F32).astype(BF16)


def back_gate_body(me, *refs, n):
    os, gs, wcat = refs[:n], refs[n : 2 * n], refs[2 * n]
    hs, gp_ref, hsc = refs[2 * n + 2 : 3 * n + 2], refs[3 * n + 2], refs[3 * n + 3]
    parts = []
    for q in range(n):
        g = gs[q][...].astype(F32)
        parts.append((os[q][...].astype(F32) * g * (1.0 - g)).astype(BF16))
    gp = lanes(parts)
    gp_ref[...] = gp
    hsc[...] = lax.dot_general(gp, wcat[...], NT, preferred_element_type=F32).astype(BF16)
    for r in range(n):
        hs[r][...] = hsc[:, pl.ds(pl.multiple_of((me[0] ^ r) * 128, 128), 128)]


def weight_body(me, xt_ref, gp_ref, mine, peer, *, n):
    g = pl.program_id(0)
    w = jnp.dot(xt_ref[...], gp_ref[...], preferred_element_type=F32).astype(BF16)

    def put(out):
        for q in range(n):
            cols = pl.ds(pl.multiple_of((me[0] ^ q) * 128, 128), 128)
            out[:, cols] = w[:, q * 128 : (q + 1) * 128]

    @pl.when(g < 2)
    def _():
        put(mine)

    @pl.when(g >= 2)
    def _():
        put(peer)


def add_body(me, a_ref, b_ref, left_ref, *outs):
    n, seqs = left_ref.shape[0], left_ref.shape[1]
    per = a_ref.shape[0] // n
    for r in range(n):
        out, base = outs[r % len(outs)], (r // len(outs)) * (per + seqs)
        rows = slice(r * per, (r + 1) * per)
        both = a_ref[rows, :].astype(F32) + b_ref[rows, :].astype(F32)
        out[base : base + per, :] = both.astype(BF16)
        out[base + per : base + per + seqs, :] = left_ref[r]


def mid_body(me, *refs, ways):
    keep, send = refs[2 * ways :]
    low = 0
    for group in (refs[:ways], refs[ways : 2 * ways]):
        size = group[0].shape[0] // 2
        keep[low : low + size, :] = total([p[:size, :] for p in group])
        send[low : low + size, :] = total([p[size:, :] for p in group]).astype(BF16)
        low += size


def row_order(me, block, n, seqs):
    rho = lax.broadcasted_iota(jnp.int32, (block, block), 0)
    col = lax.broadcasted_iota(jnp.int32, (block, block), 1)
    per = block // n
    own = per // seqs
    inner = lax.rem(rho, per)
    want = (lax.rem(inner, seqs) * n + (me[0] ^ (rho // per))) * own + inner // seqs
    return jnp.where(want == col, 1.0, 0.0).astype(BF16)


def put_rows(me, acc, n, seqs, put):
    block = acc.shape[0]
    sums = jnp.dot(
        row_order(me, block, n, seqs), acc[...].astype(BF16), preferred_element_type=F32
    ).astype(BF16)
    per = block // n
    for r in range(n):
        for t in range(per // seqs):
            for m in range(block // 128):
                slot = t * (block // 128) + m
                low = r * per + t * seqs
                put(r, slot * 128, sums[low : low + seqs, m * 128 : (m + 1) * 128])


def gate_pick(t, gs, gsc):
    for q in range(len(gs)):

        @pl.when(t == q)
        def _(q=q):
            gsc[...] = gs[q][...]


def grad_mixed_of(og_ref, gsc, block):
    return lanes(
        [
            (og_ref[u].astype(F32) * gsc[u * block : (u + 1) * block, :].astype(F32)).astype(BF16)
            for u in range(2)
        ]
    )


def cot_body(me, *refs, n):
    gs, og_ref, lt_ref, tie, gv_ref, gm_ref, gsc = refs[:n], *refs[n:]
    block = lt_ref.shape[0]
    gate_pick(pl.program_id(0), gs, gsc)
    gm = grad_mixed_of(og_ref, gsc, block)
    gm_ref[...] = gm
    gv = jnp.dot(lt_ref[...], gm, preferred_element_type=F32).astype(BF16)
    for u in range(2):
        gv_ref[:, u] = gv[:, u * 128 : (u + 1) * 128].reshape(gv_ref.shape[0], gv_ref.shape[2], 128)


def accumulate(acc, t, add):
    @pl.when(t == 0)
    def _():
        acc[...] = add

    @pl.when(t > 0)
    def _():
        acc[...] += add


def left_body(me, gm_ref, p_ref, tie, out, acc, *, n, seqs):
    t = pl.program_id(0)
    block = acc.shape[0]
    pairs = gm_ref.shape[0]
    gm = lanes([gm_ref[v] for v in range(pairs)])
    piece = lanes([p_ref[:, u].reshape(block, 128) for u in range(2 * pairs)])
    accumulate(acc, t, lax.dot_general(gm, piece, NT, preferred_element_type=F32))

    @pl.when(t == pl.num_programs(0) - 1)
    def _():
        def put(r, low, value):
            out[r, :, low : low + 128] = value

        put_rows(me, acc, n, seqs, put)


def kernel_grad_body(me, d_ref, u_ref, k_ref, x_ref, kg_ref, gu_ref, *refs, heads, n, seqs):
    outs, scr, acc = refs[:-2], refs[-2], refs[-1]
    t = pl.program_id(0)
    step, block = u_ref.shape[0], u_ref.shape[1]

    @pl.when(t == 0)
    def _():
        def get(s, carry):
            rows = d_ref[s].astype(F32).reshape(heads * heads, 128)
            scr[pl.ds(pl.multiple_of(s * heads * heads, 256), heads * heads), :] = rows
            return carry

        lax.fori_loop(0, d_ref.shape[0], get, 0)

    gus = []
    for u in range(step):
        gv = scr[pl.ds(t * step + u, block, stride=heads), :]
        kg_ref[u] = (gv * u_ref[u].astype(F32)).astype(BF16)
        gu = (gv * k_ref[u].astype(F32)).astype(BF16)
        gu_ref[u] = gu
        gus.append(gu)
    accumulate(
        acc,
        t,
        lax.dot_general(
            lanes(gus), lanes([x_ref[u] for u in range(step)]), NT, preferred_element_type=F32
        ),
    )

    @pl.when(t == pl.num_programs(0) - 1)
    def _():
        def put(r, low, value):
            base = (r // len(outs)) * seqs
            outs[r % len(outs)][base : base + seqs, low : low + 128] = value

        put_rows(me, acc, n, seqs, put)


def input_grad_body(me, *refs, n):
    hs, gu_ref, rt_ref, out, hsc = refs[:n], refs[n], refs[n + 1], refs[n + 2], refs[n + 3]
    block = rt_ref.shape[0]
    gate_pick(pl.program_id(0), hs, hsc)
    rhs = lanes([gu_ref[u] for u in range(2)])
    back = jnp.dot(rt_ref[...], rhs, preferred_element_type=F32)
    for u in range(2):
        rows = slice(u * block, (u + 1) * block)
        out[rows, :] = (back[:, u * 128 : (u + 1) * 128] + hsc[rows, :].astype(F32)).astype(BF16)


def total(parts):
    return functools.reduce(lambda a, b: a + b, [p.astype(F32) for p in parts])


def pack_body(me, keep, got, out, scr, *, seqs, per):
    slots = out.shape[1]
    sums = keep[...] + got[...].astype(F32)
    weight, left, right = sums[:per], sums[per : per + seqs], sums[per + seqs :]
    blocks = sums.shape[1] // 128
    for slot in range(blocks):
        cols = slice(slot * 128, (slot + 1) * 128)
        scr[pl.ds(slot, seqs, stride=slots), :] = left[:, cols]
        scr[pl.ds(blocks + slot, seqs, stride=slots), :] = right[:, cols]
    high = seqs // 2
    zero = jnp.zeros((high, 128), F32)
    for t in range(per // high):
        for m in range(blocks):
            slot = 2 * blocks + t * blocks + m
            value = weight[t * high : (t + 1) * high, m * 128 : (m + 1) * 128]
            scr[pl.ds(slot + me[1] * slots, high, stride=2 * slots), :] = value
            scr[pl.ds(slot + (1 - me[1]) * slots, high, stride=2 * slots), :] = zero

    def emit(s, carry):
        out[s] = scr[pl.ds(pl.multiple_of(s * slots, 16), slots), :].astype(BF16)
        return carry

    lax.fori_loop(0, seqs, emit, 0)


def share_body(me, p_ref, left_ref, right_ref, weight_ref, *, factor, token):
    sums = lax.fori_loop(
        1, p_ref.shape[0], lambda s, acc: acc + p_ref[s].astype(F32), p_ref[0].astype(F32)
    )
    count = left_ref.shape[0]
    left_ref[...] = sums[:count] * factor
    right_ref[...] = sums[count : 2 * count] * factor
    weight_ref[...] = sums[2 * count :] * token


def local(inputs, out_grad, kernel, gate_weight, right_factor, left_factor):
    block = right_factor.shape[0]
    rows, width = inputs.shape
    model_width = gate_weight.shape[0]
    heads = rows // block
    seqs = block // heads
    n = model_width // width
    part = rows // n
    chan = lax.axis_index("chan")
    seq = lax.axis_index("seq")
    core, side = seq % 2, (seq // 2) % 2
    pre = jnp.stack([chan, core, side]).astype(jnp.int32)
    S = jax.ShapeDtypeStruct

    def swap(r, x):
        return x if r == 0 else lax.ppermute(x, "chan", [(i, i ^ r) for i in range(n)])

    def swaps(parts):
        return [swap(r, parts[r]) for r in range(n)]

    def across(x, bit=1):
        return lax.ppermute(x, "seq", [(i, i ^ bit) for i in range(seqs)])

    def whole(*shape):
        return pl.BlockSpec(shape, lambda t, me: (0,) * len(shape))

    tie = pl.BlockSpec(memory_space=pl.ANY)
    mm = 2 * rows * block * width
    gg = 2 * part * model_width * model_width
    cube = rows * width * 2

    xs = lax.all_to_all(
        inputs.reshape(n, part, width), "chan", split_axis=0, concat_axis=0, tiled=True
    )
    quarter = model_width // 4
    slab = lax.dynamic_slice_in_dim(gate_weight, (core * 2 + side) * quarter, quarter, 0)
    ways = n // 2
    slabs = jnp.stack([slab, swap(ways, slab)])
    near = jnp.stack([swap(r, slabs) for r in range(ways)])
    beside = across(near, 2)
    quads = [near, beside, across(near), across(beside)]

    x_cube = inputs.reshape(heads, block, width)
    og_cube = out_grad.reshape(heads, block, width)
    step = 4
    four = pl.BlockSpec((step, block, width), lambda g, me: (g, 0, 0))
    first, scaled = call(
        functools.partial(first_body, step=step), (heads // step,),
        [four, four, whole(block, block)],
        [four, whole(seqs, heads, heads, width)],
        [S((heads, block, width), BF16), S((seqs, heads, heads, width), BF16)],
        [pltpu.VMEM((block * heads, width), F32)],
        mm, 4 * cube,
    )(pre, x_cube, kernel, right_factor)
    piece = lax.all_to_all(scaled, "seq", split_axis=0, concat_axis=0, tiled=True)

    chunk = part // 4
    tok = pl.BlockSpec((chunk, width), lambda t, me: (t, 0))
    gate_out = call(
        functools.partial(gate_body, n=n), (part // chunk,),
        [
            pl.BlockSpec((n, chunk, width), lambda t, me: (0, t, 0)),
        ]
        + [whole(n // 2, 2, model_width // 4, width)] * 4,
        [tok] * n + [whole(model_width, model_width)],
        [S((part, width), BF16)] * n + [S((model_width, model_width), BF16)],
        [pltpu.VMEM((model_width, model_width), BF16)],
        gg, 4 * cube,
    )(pre, xs, *quads)
    gates_tok, wcat = gate_out[:n], gate_out[n]
    gates = swaps(gates_tok)

    pair_in = pl.BlockSpec((seqs, 2, heads, width), lambda t, me: (0, me[0] ^ t, 0, 0))
    pair_cube = pl.BlockSpec((2, block, width), lambda t, me: (me[0] ^ t, 0, 0))
    om = call(
        mix_body, (n,),
        [pair_in, pair_cube, whole(block, block)],
        [whole(part, width)] * n,
        [S((part, width), BF16)] * n,
        [],
        mm, 3 * cube,
    )(pre, piece, og_cube, left_factor)
    oms = swaps(om)

    grad_mid, grad_mixed = call(
        functools.partial(cot_body, n=n), (n,),
        [whole(part, width)] * n + [pair_cube, whole(block, block), tie],
        [pair_in, pl.BlockSpec((None, block, 2 * width), lambda t, me: (me[0] ^ t, 0, 0))],
        [S((seqs, heads, heads, width), BF16), S((n, block, 2 * width), BF16)],
        [pltpu.VMEM((part, width), BF16)],
        mm, 4 * cube,
    )(pre, *gates, og_cube, left_factor.T, om[0])
    grad_back = lax.all_to_all(grad_mid, "seq", split_axis=0, concat_axis=0, tiled=True)

    count = block * block // (n * seqs * 128)
    lefts = call(
        functools.partial(left_body, n=n, seqs=seqs), (n // 2,),
        [
            pl.BlockSpec((2, block, 2 * width), lambda t, me: (t, 0, 0)),
            pl.BlockSpec((seqs, 4, heads, width), lambda t, me: (0, t, 0, 0)),
            tie,
        ],
        whole(n, seqs, count * 128),
        S((n, seqs, count * 128), BF16),
        [pltpu.VMEM((block, block), F32)],
        mm, 2 * cube,
    )(pre, grad_mixed, piece, om[0])

    turned = call(
        functools.partial(turn_body, n=n, seqs=seqs), (4,),
        [whole(n, part, width)],
        pl.BlockSpec((model_width // 4, part), lambda t, me: (t, 0)),
        S((model_width, part), BF16),
        [],
        gg, 2 * cube,
    )(pre, xs)

    back_out = call(
        functools.partial(back_gate_body, n=n), (part // chunk,),
        [tok] * n + [tok] * n + [whole(model_width, model_width), tie],
        [tok] * n + [pl.BlockSpec((chunk, model_width), lambda t, me: (t, 0))],
        [S((part, width), BF16)] * n + [S((part, model_width), BF16)],
        [pltpu.VMEM((chunk, model_width), BF16)],
        gg, 5 * cube,
    )(pre, *oms, *gates_tok, wcat, lefts)
    grad_pre = back_out[n]

    strip = (model_width // 4, model_width)
    mine, other = call(
        functools.partial(weight_body, n=n), (4,),
        [
            pl.BlockSpec((model_width // 4, part), lambda t, me: (t, 0)),
            whole(part, model_width),
        ],
        [
            pl.BlockSpec(strip, lambda t, me: (jnp.minimum(t, 1), 0)),
            pl.BlockSpec(strip, lambda t, me: (jnp.maximum(t - 2, 0), 0)),
        ],
        [S((model_width // 2, model_width), BF16)] * 2,
        [],
        gg, 3 * cube,
    )(pre, turned, grad_pre)
    per = model_width // (2 * n)
    size = per + seqs
    sums_out = call(
        add_body, (1,),
        [whole(model_width // 2, model_width)] * 2 + [whole(n, seqs, count * 128)],
        [whole(2 * size, model_width)] * ways,
        [S((2 * size, model_width), BF16)] * ways,
        [],
        cube, 2 * cube,
    )(pre, mine, across(other), lefts)
    sums = [swap(r, sums_out[r]) for r in range(ways)]
    hs = swaps(back_out[:n])

    kernel_out = call(
        functools.partial(kernel_grad_body, heads=heads, n=n, seqs=seqs), (heads // step,),
        [whole(seqs, heads, heads, width), four, four, four],
        [four, four] + [whole(2 * seqs, count * 128)] * ways,
        [S((heads, block, width), BF16)] * 2 + [S((2 * seqs, count * 128), BF16)] * ways,
        [pltpu.VMEM((block * heads, width), F32), pltpu.VMEM((block, block), F32)],
        mm, 6 * cube,
    )(pre, grad_back, first, kernel, x_cube)

    kernel_grad, grad_first = kernel_out[:2]
    rights = [swap(r, kernel_out[2 + r]) for r in range(ways)]
    whole_size = size + seqs
    keep, send = call(
        functools.partial(mid_body, ways=ways), (1,),
        [whole(2 * size, model_width)] * ways + [whole(2 * seqs, model_width)] * ways,
        [whole(whole_size, model_width)] * 2,
        [S((whole_size, model_width), F32), S((whole_size, model_width), BF16)],
        [],
        cube, 2 * cube,
    )(pre, *sums, *rights)

    slots = 2 * count + model_width * model_width // (n * seqs * 128)
    packed = call(
        functools.partial(pack_body, seqs=seqs, per=per), (1,),
        [whole(whole_size, model_width)] * 2,
        whole(seqs, slots, 128),
        S((seqs, slots, 128), BF16),
        [pltpu.VMEM((seqs * slots, 128), F32)],
        cube, cube,
    )(pre, keep, swap(ways, send))
    got = lax.all_to_all(packed, "seq", split_axis=0, concat_axis=0, tiled=True)

    input_grad = call(
        functools.partial(input_grad_body, n=n), (n,),
        [whole(part, width)] * n + [pair_cube, whole(block, block)],
        pl.BlockSpec((part, width), lambda t, me: (me[0] ^ t, 0)),
        S((rows, width), BF16),
        [pltpu.VMEM((part, width), BF16)],
        mm, 3 * cube,
    )(pre, *hs, grad_first, right_factor.T)

    left_share, right_share, weight_share = call(
        functools.partial(
            share_body, factor=(block * model_width) ** -0.5, token=1.0 / block
        ), (1,),
        [whole(seqs, slots, 128)],
        [whole(count, 128), whole(count, 128), whole(slots - 2 * count, 128)],
        [S((count, 128), F32), S((count, 128), F32), S((slots - 2 * count, 128), F32)],
        [],
        cube, cube,
    )(pre, got)
    return (
        input_grad,
        kernel_grad,
        right_share.reshape(-1),
        left_share.reshape(-1),
        weight_share.reshape(-1, model_width),
    )


def solution(mesh):
    in_specs = (
        P("seq", "chan"),
        P("seq", "chan"),
        P("seq", None, "chan"),
        P(None, "chan"),
        P(),
        P(),
    )
    out_specs = (
        P("seq", "chan"),
        P("seq", None, "chan"),
        P(("seq", "chan")),
        P(("seq", "chan")),
        P(("seq", "chan"), None),
    )
    return jax.shard_map(
        local, mesh=mesh, in_specs=in_specs, out_specs=out_specs, check_vma=False
    )
```

profile of v0, /device:TPU:2, one launch (start us, length us, event | category | flops | bytes accessed | tf_op | source)
XLA Modules:
  0.0 340.4 jit_solution(2270396454564233074)
XLA Ops:
  0.7 6.2 %all-to-all-start.1 = ((bf16[8,1024,128]{2,1,0:T(8,128)(2,1)}), bf16[8,1024,128]{2,1,0:T(8,128)(2,1)S(1)}, u32[]{:S(2)}, u32[]{:S(2)}) async-start(bf16[8,1024,128]{2,1,0:T(8,128)(2,1)} %bitcast.20), calls=%async_computation.1 | async-start | bytes 4194304 | tf_op jit(solution)/shard_map/all_to_all | solution.py:362
  6.9 5.4 %shard_map.101 = (bf16[16,512,128]{2,1,0:T(8,128)(2,1)S(1)}, bf16[32,16,16,128]{3,2,1,0:T(8,128)(2,1)S(1)}) custom-call(s32[3]{0:T(128)S(1)} %pad_add_fusion.me, bf16[16,512,128]{2,1,0:T(8,128)(2,1)} %bitcast.21, bf16[16,512,128]{2,1,0:T(8,128)(2,1)} %k_ref.3, bf16[512,512]{1,0:T(8,128)(2,1)S(1)} %copy-done.2), custom_call_target="tpu_custom_call" | custom-call | flops 1073741824 | bytes 8388608 | tf_op jit(solution)/shard_map/pallas_call | solution.py:377
  15.0 18.3 %all-to-all-done.1.x_ref = bf16[8,1024,128]{2,1,0:T(8,128)(2,1)S(1)} async-done(((bf16[8,1024,128]{2,1,0:T(8,128)(2,1)}), bf16[8,1024,128]{2,1,0:T(8,128)(2,1)S(1)}, u32[]{:S(2)}, u32[]{:S(2)}) %all-to-all-start.1) | async-done | bytes 2097184 | tf_op jit(solution)/shard_map/all_to_all | solution.py:362
  34.6 10.1 %all-to-all-start = ((bf16[32,16,16,128]{3,2,1,0:T(8,128)(2,1)}), bf16[32,16,16,128]{3,2,1,0:T(8,128)(2,1)S(1)}, u32[]{:S(2)}, u32[]{:S(2)}) async-start(bf16[32,16,16,128]{3,2,1,0:T(8,128)(2,1)} %copy-done.6), calls=%async_computation | async-start | bytes 4194304 | tf_op jit(solution)/shard_map/all_to_all | solution.py:385
  47.4 7.2 %collective-permute-done.7 = bf16[256,128]{1,0:T(8,128)(2,1)S(1)} collective-permute-done((bf16[256,128]{1,0:T(8,128)(2,1)S(1)}, bf16[256,128]{1,0:T(8,128)(2,1)S(1)}, u32[]{:S(2)}, u32[]{:S(2)}) %collective-permute-start.7) | collective-permute-done | bytes 65568 | tf_op jit(solution)/shard_map/ppermute | solution.py:346
  64.7 38.7 %collective-permute-done.11.refs_1_ = bf16[4,2,256,128]{3,2,1,0:T(8,128)(2,1)S(1)} collective-permute-done((bf16[4,2,256,128]{3,2,1,0:T(8,128)(2,1)S(1)}, bf16[4,2,256,128]{3,2,1,0:T(8,128)(2,1)S(1)}, u32[]{:S(2)}, u32[]{:S(2)}) %collective-permute-start.11) | collective-permute-done | bytes 524320 | tf_op jit(solution)/shard_map/ppermute | solution.py:352
  105.3 6.9 %shard_map.103 = (bf16[1024,128]{1,0:T(8,128)(2,1)S(1)}, bf16[1024,128]{1,0:T(8,128)(2,1)S(1)}, bf16[1024,128]{1,0:T(8,128)(2,1)S(1)}, bf16[1024,128]{1,0:T(8,12...) custom-call(s32[3]{0:T(128)S(1)} %pad_add_fusion.me, ...), custom_call_target="tpu_custom_call" | custom-call | flops 2147483648 | bytes 8388608 | tf_op jit(solution)/shard_map/pallas_call | solution.py:389
  122.9 4.7 %collective-permute-start.19 = (bf16[1024,128]{1,0:T(8,128)(2,1)}, bf16[1024,128]{1,0:T(8,128)(2,1)}, u32[]{:S(2)}, u32[]{:S(2)}) collective-permute-start(bf16[1024,128]{1,0:T(8,128)(2,1)} %get-tuple-element.67.refs_14_), channel_id=1, source_target_pairs={{0,6},{1,7},{2,4},{3,5},{4,2},{5,3},{6,0},{7,1},{8,14},{9,15},{10,... | collective-permute-start | bytes 786440 | tf_op jit(solution)/shard_map/ppermute | solution.py:346
  127.6 3.3 collective-permute-done.15.refs_2_
  134.6 6.4 %shard_map.102 = (bf16[1024,128]{1,0:T(8,128)(2,1)S(1)}, bf16[1024,128]{1,0:T(8,128)(2,1)S(1)}, bf16[1024,128]{1,0:T(8,128)(2,1)S(1)}, bf16[1024,128]{1,0:T(8,12...) custom-call(s32[3]{0:T(128)S(1)} %pad_add_fusion.me, ...), custom_call_target="tpu_custom_call" | custom-call | flops 1073741824 | bytes 6291456 | tf_op jit(solution)/shard_map/pallas_call | solution.py:405
  147.6 8.0 %shard_map.104 = (bf16[32,16,16,128]{3,2,1,0:T(8,128)(2,1)S(1)}, bf16[8,512,256]{2,1,0:T(8,128)(2,1)}) custom-call(s32[3]{0:T(128)S(1)} %pad_add_fusion.me, bf16[1024,128]{1,0:T(8,128)(2,1)S(1)} %copy-done.17, bf16[1024,128]{1,0:T(8,128)(2,1)S(1)} %copy-done.20, bf16[1024,128]{1,0:T(8,128)(2,1)S(1)} %copy-done.22, ...), custom_call_target="tpu_custom_call" | custom-call | flops 1073741824 | bytes 8388608 | tf_op jit(solution)/shard_map/pallas_call | solution.py:415
  156.9 7.6 %all-to-all-start.2 = ((bf16[32,16,16,128]{3,2,1,0:T(8,128)(2,1)}), bf16[32,16,16,128]{3,2,1,0:T(8,128)(2,1)}, u32[]{:S(2)}, u32[]{:S(2)}) async-start(bf16[32,16,16,128]{3,2,1,0:T(8,128)(2,1)} %copy-done.7), calls=%async_computation.2 | async-start | bytes 4194304 | tf_op jit(solution)/shard_map/all_to_all | solution.py:423
  165.5 9.5 %collective-permute-start.1 = (bf16[1024,128]{1,0:T(8,128)(2,1)}, bf16[1024,128]{1,0:T(8,128)(2,1)S(1)}, u32[]{:S(2)}, u32[]{:S(2)}) collective-permute-start(bf16[1024,128]{1,0:T(8,128)(2,1)} %copy-done.53), channel_id=1, source_target_pairs={{0,2},{1,3},{2,0},{3,1},{4,6},{5,7},{6,4},{7,5},{8,10},{9,11},{10,... | collective-permute-start | bytes 786440 | tf_op jit(solution)/shard_map/ppermute | solution.py:346
  177.9 4.2 %collective-permute-start.5 = (bf16[1024,128]{1,0:T(8,128)(2,1)S(1)}, bf16[1024,128]{1,0:T(8,128)(2,1)S(1)}, u32[]{:S(2)}, u32[]{:S(2)}) collective-permute-start(bf16[1024,128]{1,0:T(8,128)(2,1)S(1)} %copy-done.49), channel_id=1, source_target_pairs={{0,6},{1,7},{2,4},{3,5},{4,2},{5,3},{6,0},{7,1},{8,14},{9,15},{10,... | collective-permute-start | bytes 786440 | tf_op jit(solution)/shard_map/ppermute | solution.py:346
  182.1 5.2 %collective-permute-done.1.refs_2_ = bf16[1024,128]{1,0:T(8,128)(2,1)S(1)} collective-permute-done((bf16[1024,128]{1,0:T(8,128)(2,1)}, bf16[1024,128]{1,0:T(8,128)(2,1)S(1)}, u32[]{:S(2)}, u32[]{:S(2)}) %collective-permute-start.1) | collective-permute-done | bytes 262176 | tf_op jit(solution)/shard_map/ppermute | solution.py:346
  188.9 4.3 %shard_map.109.xt_ref = bf16[1024,1024]{1,0:T(8,128)(2,1)S(1)} custom-call(s32[3]{0:T(128)S(1)} %pad_add_fusion.me, bf16[8,1024,128]{2,1,0:T(8,128)(2,1)S(1)} %copy-done.5), custom_call_target="tpu_custom_call" | custom-call | flops 2147483648 | bytes 4194304 | tf_op jit(solution)/shard_map/pallas_call | solution.py:439
  193.3 3.4 %shard_map.105.refs_17_.left_ref = bf16[8,32,1024]{2,1,0:T(8,128)(2,1)S(1)} custom-call(s32[3]{0:T(128)S(1)} %pad_add_fusion.me, bf16[8,512,256]{2,1,0:T(8,128)(2,1)S(1)} %copy-done.10, bf16[32,16,16,128]{3,2,1,0:T(8,128)(2,1)S(1)} %all-to-all-done.p_ref, bf16[1024,128]{1,0:T(8,128)(2,1)S(1)} %copy-done.15), custom_call_target="tpu_custom_call" | custom-call | flops 1073741824 | bytes 4194304 | tf_op jit(solution)/shard_map/pallas_call | solution.py:426
  199.8 11.2 %collective-permute-done.5.refs_6_ = bf16[1024,128]{1,0:T(8,128)(2,1)S(1)} collective-permute-done((bf16[1024,128]{1,0:T(8,128)(2,1)S(1)}, bf16[1024,128]{1,0:T(8,128)(2,1)S(1)}, u32[]{:S(2)}, u32[]{:S(2)}) %collective-permute-start.5) | collective-permute-done | bytes 262176 | tf_op jit(solution)/shard_map/ppermute | solution.py:346
  211.0 7.3 %collective-permute-done.6.refs_7_ = bf16[1024,128]{1,0:T(8,128)(2,1)S(1)} collective-permute-done((bf16[1024,128]{1,0:T(8,128)(2,1)S(1)}, bf16[1024,128]{1,0:T(8,128)(2,1)S(1)}, u32[]{:S(2)}, u32[]{:S(2)}) %collective-permute-start.6) | collective-permute-done | bytes 262176 | tf_op jit(solution)/shard_map/ppermute | solution.py:346
  218.3 6.3 %shard_map.106 = (bf16[1024,128]{1,0:T(8,128)(2,1)S(1)}, bf16[1024,128]{1,0:T(8,128)(2,1)S(1)}, bf16[1024,128]{1,0:T(8,128)(2,1)S(1)}, bf16[1024,128]{1,0:T(8,12...) custom-call(s32[3]{0:T(128)S(1)} %pad_add_fusion.me, ...), custom_call_target="tpu_custom_call" | custom-call | flops 2147483648 | bytes 10485760 | tf_op jit(solution)/shard_map/pallas_call | solution.py:448
  229.6 5.5 %shard_map.110 = (bf16[512,1024]{1,0:T(8,128)(2,1)S(1)}, bf16[512,1024]{1,0:T(8,128)(2,1)S(1)}) custom-call(s32[3]{0:T(128)S(1)} %pad_add_fusion.me, bf16[1024,1024]{1,0:T(8,128)(2,1)S(1)} %shard_map.109.xt_ref, bf16[1024,1024]{1,0:T(8,128)(2,1)} %get-tuple-element.83.gp_ref), custom_call_target="tpu_custom_call" | custom-call | flops 2147483648 | bytes 6291456 | tf_op jit(solution)/shard_map/pallas_call | solution.py:459
  239.6 4.3 %collective-permute-start.30 = (bf16[192,1024]{1,0:T(8,128)(2,1)}, bf16[192,1024]{1,0:T(8,128)(2,1)}, u32[]{:S(2)}, u32[]{:S(2)}) collective-permute-start(bf16[192,1024]{1,0:T(8,128)(2,1)} %get-tuple-element.88), channel_id=1, source_target_pairs={{0,2},{1,3},{2,0},{3,1},{4,6},{5,7},{6,4},{7,5},{8,10},{9,11},{10,... | collective-permute-start | bytes 1179656 | tf_op jit(solution)/shard_map/ppermute | solution.py:346
  244.3 8.2 %shard_map.107 = (bf16[16,512,128]{2,1,0:T(8,128)(2,1)}, bf16[16,512,128]{2,1,0:T(8,128)(2,1)S(1)}, bf16[64,1024]{1,0:T(8,128)(2,1)S(1)}, bf16[64,1024]{1,0:T(8,...) custom-call(s32[3]{0:T(128)S(1)} %pad_add_fusion.me, ...), custom_call_target="tpu_custom_call" | custom-call | flops 1073741824 | bytes 12582912 | tf_op jit(solution)/shard_map/pallas_call | solution.py:486
  253.8 4.3 %collective-permute-start.33 = (bf16[64,1024]{1,0:T(8,128)(2,1)S(1)}, bf16[64,1024]{1,0:T(8,128)(2,1)S(1)}, u32[]{:S(2)}, u32[]{:S(2)}) collective-permute-start(bf16[64,1024]{1,0:T(8,128)(2,1)S(1)} %get-tuple-element.92), channel_id=1, source_target_pairs={{0,2},{1,3},{2,0},{3,1},{4,6},{5,7},{6,4},{7,5},{8,10},{9,11},{10,... | collective-permute-start | bytes 393224 | tf_op jit(solution)/shard_map/ppermute | solution.py:346
  258.5 4.2 %collective-permute-done.30.refs_2_ = bf16[192,1024]{1,0:T(8,128)(2,1)} collective-permute-done((bf16[192,1024]{1,0:T(8,128)(2,1)}, bf16[192,1024]{1,0:T(8,128)(2,1)}, u32[]{:S(2)}, u32[]{:S(2)}) %collective-permute-start.30) | collective-permute-done | bytes 393248 | tf_op jit(solution)/shard_map/ppermute | solution.py:346
  262.6 6.0 %collective-permute-done.31.refs_3_ = bf16[192,1024]{1,0:T(8,128)(2,1)} collective-permute-done((bf16[192,1024]{1,0:T(8,128)(2,1)}, bf16[192,1024]{1,0:T(8,128)(2,1)}, u32[]{:S(2)}, u32[]{:S(2)}) %collective-permute-start.31) | collective-permute-done | bytes 393248 | tf_op jit(solution)/shard_map/ppermute | solution.py:346
  272.7 7.8 %collective-permute-done.35.got = bf16[128,1024]{1,0:T(8,128)(2,1)S(1)} collective-permute-done((bf16[128,1024]{1,0:T(8,128)(2,1)S(1)}, bf16[128,1024]{1,0:T(8,128)(2,1)S(1)}, u32[]{:S(2)}, u32[]{:S(2)}) %collective-permute-start.35) | collective-permute-done | bytes 262176 | tf_op jit(solution)/shard_map/ppermute | solution.py:346
  282.6 8.3 %all-to-all-start.3 = ((bf16[32,48,128]{2,1,0:T(8,128)(2,1)}), bf16[32,48,128]{2,1,0:T(8,128)(2,1)S(1)}, u32[]{:S(2)}, u32[]{:S(2)}) async-start(bf16[32,48,128]{2,1,0:T(8,128)(2,1)} %shard_map.113), calls=%async_computation.3 | async-start | bytes 786432 | tf_op jit(solution)/shard_map/all_to_all | solution.py:516
  300.4 3.5 %collective-permute-start.26 = (bf16[1024,128]{1,0:T(8,128)(2,1)}, bf16[1024,128]{1,0:T(8,128)(2,1)S(1)}, u32[]{:S(2)}, u32[]{:S(2)}) collective-permute-start(bf16[1024,128]{1,0:T(8,128)(2,1)} %copy-done.36), channel_id=1, source_target_pairs={{0,6},{1,7},{2,4},{3,5},{4,2},{5,3},{6,0},{7,1},{8,14},{9,15},{10,... | collective-permute-start | bytes 786440 | tf_op jit(solution)/shard_map/ppermute | solution.py:346
  312.9 5.9 %collective-permute-done.26.refs_6_ = bf16[1024,128]{1,0:T(8,128)(2,1)S(1)} collective-permute-done((bf16[1024,128]{1,0:T(8,128)(2,1)}, bf16[1024,128]{1,0:T(8,128)(2,1)S(1)}, u32[]{:S(2)}, u32[]{:S(2)}) %collective-permute-start.26) | collective-permute-done | bytes 262176 | tf_op jit(solution)/shard_map/ppermute | solution.py:346
  319.5 5.7 %collective-permute-done.27.refs_7_ = bf16[1024,128]{1,0:T(8,128)(2,1)} collective-permute-done((bf16[1024,128]{1,0:T(8,128)(2,1)}, bf16[1024,128]{1,0:T(8,128)(2,1)}, u32[]{:S(2)}, u32[]{:S(2)}) %collective-permute-start.27) | collective-permute-done | bytes 262176 | tf_op jit(solution)/shard_map/ppermute | solution.py:346
  332.4 6.0 %shard_map.108 = bf16[8192,128]{1,0:T(8,128)(2,1)} custom-call(s32[3]{0:T(128)S(1)} %pad_add_fusion.me, bf16[1024,128]{1,0:T(8,128)(2,1)S(1)} %get-tuple-element.71.refs_0_, bf16[1024,128]{1,0:T(8,128)(2,1)S(1)} %copy-done.24, bf16[1024,128]{1,0:T(8,128)(2,1)S(1)} %copy-done.26, bf16[1024,128]{1,0:T(8,128)(2,1)S(1)} %copy-done.28, ...), custom_call_target="tpu_custom_call" | custom-call | flops 1073741824 | bytes 6291456 | tf_op jit(solution)/shard_map/pallas_call | solution.py:518
  (180 shorter events, 95.4 us)
Async XLA Ops:
  0.7 32.6 %all-to-all-start.1 = ((bf16[8,1024,128]{2,1,0:T(8,128)(2,1)}), bf16[8,1024,128]{2,1,0:T(8,128)(2,1)S(1)}, u32[]{:S(2)}, u32[]{:S(2)}) async-start(bf16[8,1024,128]{2,1,0:T(8,128)(2,1)} %bitcast.20), calls=%async_computation.1 | async-start | bytes 4194304 | tf_op jit(solution)/shard_map/all_to_all | solution.py:362
  34.6 100.0 %all-to-all-start = ((bf16[32,16,16,128]{3,2,1,0:T(8,128)(2,1)}), bf16[32,16,16,128]{3,2,1,0:T(8,128)(2,1)S(1)}, u32[]{:S(2)}, u32[]{:S(2)}) async-start(bf16[32,16,16,128]{3,2,1,0:T(8,128)(2,1)} %copy-done.6), calls=%async_computation | async-start | bytes 4194304 | tf_op jit(solution)/shard_map/all_to_all | solution.py:385
  44.7 9.9 %collective-permute-start.7 = (bf16[256,128]{1,0:T(8,128)(2,1)S(1)}, bf16[256,128]{1,0:T(8,128)(2,1)S(1)}, u32[]{:S(2)}, u32[]{:S(2)}) collective-permute-start(bf16[256,128]{1,0:T(8,128)(2,1)S(1)} %constant_dynamic-slice_fusion), channel_id=1, source_target_pairs={{0,4},{1,5},{2,6},{3,7},{4,0},{5,1},{6,2},{7,3},{8,12},{9,13},{10,... | collective-permute-start | bytes 196616 | tf_op jit(solution)/shard_map/ppermute | solution.py:346
  63.2 40.2 %collective-permute-start.11 = (bf16[4,2,256,128]{3,2,1,0:T(8,128)(2,1)S(1)}, bf16[4,2,256,128]{3,2,1,0:T(8,128)(2,1)S(1)}, u32[]{:S(2)}, u32[]{:S(2)}) collective-permute-start(bf16[4,2,256,128]{3,2,1,0:T(8,128)(2,1)S(1)} %pad_maximum_fusion.refs_0_), channel_id=1, source_target_pairs={{0,16},{8,24},{16,0},{24,8},{32,48},{40,56},{48,32},{56,40},{64,80... | collective-permute-start | bytes 1572872 | tf_op jit(solution)/shard_map/ppermute | solution.py:352
  64.7 38.7 %collective-permute-start.12 = (bf16[4,2,256,128]{3,2,1,0:T(8,128)(2,1)S(1)}, bf16[4,2,256,128]{3,2,1,0:T(8,128)(2,1)S(1)}, u32[]{:S(2)}, u32[]{:S(2)}) collective-permute-start(bf16[4,2,256,128]{3,2,1,0:T(8,128)(2,1)S(1)} %pad_maximum_fusion.refs_0_), channel_id=1, source_target_pairs={{0,8},{8,0},{16,24},{24,16},{32,40},{40,32},{48,56},{56,48},{64,72... | collective-permute-start | bytes 1572872 | tf_op jit(solution)/shard_map/ppermute | solution.py:352
  115.0 15.9 %collective-permute-start.15 = (bf16[1024,128]{1,0:T(8,128)(2,1)S(1)}, bf16[1024,128]{1,0:T(8,128)(2,1)S(1)}, u32[]{:S(2)}, u32[]{:S(2)}) collective-permute-start(bf16[1024,128]{1,0:T(8,128)(2,1)S(1)} %get-tuple-element.63.refs_10_), channel_id=1, source_target_pairs={{0,2},{1,3},{2,0},{3,1},{4,6},{5,7},{6,4},{7,5},{8,10},{9,11},{10,... | collective-permute-start | bytes 786440 | tf_op jit(solution)/shard_map/ppermute | solution.py:346
  118.7 27.2 %collective-permute-start.16 = (bf16[1024,128]{1,0:T(8,128)(2,1)}, bf16[1024,128]{1,0:T(8,128)(2,1)}, u32[]{:S(2)}, u32[]{:S(2)}) collective-permute-start(bf16[1024,128]{1,0:T(8,128)(2,1)} %get-tuple-element.64.refs_11_), channel_id=1, source_target_pairs={{0,3},{1,2},{2,1},{3,0},{4,7},{5,6},{6,5},{7,4},{8,11},{9,10},{10,... | collective-permute-start | bytes 786440 | tf_op jit(solution)/shard_map/ppermute | solution.py:346
  119.0 27.0 %collective-permute-start.17 = (bf16[1024,128]{1,0:T(8,128)(2,1)}, bf16[1024,128]{1,0:T(8,128)(2,1)}, u32[]{:S(2)}, u32[]{:S(2)}) collective-permute-start(bf16[1024,128]{1,0:T(8,128)(2,1)} %get-tuple-element.65.refs_12_), channel_id=1, source_target_pairs={{0,4},{1,5},{2,6},{3,7},{4,0},{5,1},{6,2},{7,3},{8,12},{9,13},{10,... | collective-permute-start | bytes 786440 | tf_op jit(solution)/shard_map/ppermute | solution.py:346
  121.5 24.4 %collective-permute-start.18 = (bf16[1024,128]{1,0:T(8,128)(2,1)}, bf16[1024,128]{1,0:T(8,128)(2,1)}, u32[]{:S(2)}, u32[]{:S(2)}) collective-permute-start(bf16[1024,128]{1,0:T(8,128)(2,1)} %get-tuple-element.66.refs_13_), channel_id=1, source_target_pairs={{0,5},{1,4},{2,7},{3,6},{4,1},{5,0},{6,3},{7,2},{8,13},{9,12},{10,... | collective-permute-start | bytes 786440 | tf_op jit(solution)/shard_map/ppermute | solution.py:346
  122.9 23.1 %collective-permute-start.19 = (bf16[1024,128]{1,0:T(8,128)(2,1)}, bf16[1024,128]{1,0:T(8,128)(2,1)}, u32[]{:S(2)}, u32[]{:S(2)}) collective-permute-start(bf16[1024,128]{1,0:T(8,128)(2,1)} %get-tuple-element.67.refs_14_), channel_id=1, source_target_pairs={{0,6},{1,7},{2,4},{3,5},{4,2},{5,3},{6,0},{7,1},{8,14},{9,15},{10,... | collective-permute-start | bytes 786440 | tf_op jit(solution)/shard_map/ppermute | solution.py:346
  131.6 16.0 %collective-permute-start.20 = (bf16[1024,128]{1,0:T(8,128)(2,1)}, bf16[1024,128]{1,0:T(8,128)(2,1)}, u32[]{:S(2)}, u32[]{:S(2)}) collective-permute-start(bf16[1024,128]{1,0:T(8,128)(2,1)} %get-tuple-element.68.refs_15_), channel_id=1, source_target_pairs={{0,7},{1,6},{2,5},{3,4},{4,3},{5,2},{6,1},{7,0},{8,15},{9,14},{10,... | collective-permute-start | bytes 786440 | tf_op jit(solution)/shard_map/ppermute | solution.py:346
  156.9 87.3 %all-to-all-start.2 = ((bf16[32,16,16,128]{3,2,1,0:T(8,128)(2,1)}), bf16[32,16,16,128]{3,2,1,0:T(8,128)(2,1)}, u32[]{:S(2)}, u32[]{:S(2)}) async-start(bf16[32,16,16,128]{3,2,1,0:T(8,128)(2,1)} %copy-done.7), calls=%async_computation.2 | async-start | bytes 4194304 | tf_op jit(solution)/shard_map/all_to_all | solution.py:423
  164.5 13.4 %collective-permute-start = (bf16[1024,128]{1,0:T(8,128)(2,1)}, bf16[1024,128]{1,0:T(8,128)(2,1)S(1)}, u32[]{:S(2)}, u32[]{:S(2)}) collective-permute-start(bf16[1024,128]{1,0:T(8,128)(2,1)} %copy-done.54), channel_id=1, source_target_pairs={{0,1},{1,0},{2,3},{3,2},{4,5},{5,4},{6,7},{7,6},{8,9},{9,8},{10,11... | collective-permute-start | bytes 786440 | tf_op jit(solution)/shard_map/ppermute | solution.py:346
  165.5 21.9 %collective-permute-start.1 = (bf16[1024,128]{1,0:T(8,128)(2,1)}, bf16[1024,128]{1,0:T(8,128)(2,1)S(1)}, u32[]{:S(2)}, u32[]{:S(2)}) collective-permute-start(bf16[1024,128]{1,0:T(8,128)(2,1)} %copy-done.53), channel_id=1, source_target_pairs={{0,2},{1,3},{2,0},{3,1},{4,6},{5,7},{6,4},{7,5},{8,10},{9,11},{10,... | collective-permute-start | bytes 786440 | tf_op jit(solution)/shard_map/ppermute | solution.py:346
  175.0 22.6 %collective-permute-start.2 = (bf16[1024,128]{1,0:T(8,128)(2,1)}, bf16[1024,128]{1,0:T(8,128)(2,1)S(1)}, u32[]{:S(2)}, u32[]{:S(2)}) collective-permute-start(bf16[1024,128]{1,0:T(8,128)(2,1)} %copy-done.52), channel_id=1, source_target_pairs={{0,3},{1,2},{2,1},{3,0},{4,7},{5,6},{6,5},{7,4},{8,11},{9,10},{10,... | collective-permute-start | bytes 786440 | tf_op jit(solution)/shard_map/ppermute | solution.py:346
  175.0 22.6 %collective-permute-start.3 = (bf16[1024,128]{1,0:T(8,128)(2,1)}, bf16[1024,128]{1,0:T(8,128)(2,1)S(1)}, u32[]{:S(2)}, u32[]{:S(2)}) collective-permute-start(bf16[1024,128]{1,0:T(8,128)(2,1)} %copy-done.51), channel_id=1, source_target_pairs={{0,4},{1,5},{2,6},{3,7},{4,0},{5,1},{6,2},{7,3},{8,12},{9,13},{10,... | collective-permute-start | bytes 786440 | tf_op jit(solution)/shard_map/ppermute | solution.py:346
  175.6 24.3 %collective-permute-start.4 = (bf16[1024,128]{1,0:T(8,128)(2,1)}, bf16[1024,128]{1,0:T(8,128)(2,1)S(1)}, u32[]{:S(2)}, u32[]{:S(2)}) collective-permute-start(bf16[1024,128]{1,0:T(8,128)(2,1)} %copy-done.50), channel_id=1, source_target_pairs={{0,5},{1,4},{2,7},{3,6},{4,1},{5,0},{6,3},{7,2},{8,13},{9,12},{10,... | collective-permute-start | bytes 786440 | tf_op jit(solution)/shard_map/ppermute | solution.py:346
  177.9 33.1 %collective-permute-start.5 = (bf16[1024,128]{1,0:T(8,128)(2,1)S(1)}, bf16[1024,128]{1,0:T(8,128)(2,1)S(1)}, u32[]{:S(2)}, u32[]{:S(2)}) collective-permute-start(bf16[1024,128]{1,0:T(8,128)(2,1)S(1)} %copy-done.49), channel_id=1, source_target_pairs={{0,6},{1,7},{2,4},{3,5},{4,2},{5,3},{6,0},{7,1},{8,14},{9,15},{10,... | collective-permute-start | bytes 786440 | tf_op jit(solution)/shard_map/ppermute | solution.py:346
  187.3 31.0 %collective-permute-start.6 = (bf16[1024,128]{1,0:T(8,128)(2,1)S(1)}, bf16[1024,128]{1,0:T(8,128)(2,1)S(1)}, u32[]{:S(2)}, u32[]{:S(2)}) collective-permute-start(bf16[1024,128]{1,0:T(8,128)(2,1)S(1)} %copy-done.47), channel_id=1, source_target_pairs={{0,7},{1,6},{2,5},{3,4},{4,3},{5,2},{6,1},{7,0},{8,15},{9,14},{10,... | collective-permute-start | bytes 786440 | tf_op jit(solution)/shard_map/ppermute | solution.py:346
  239.5 18.5 %collective-permute-start.29 = (bf16[192,1024]{1,0:T(8,128)(2,1)}, bf16[192,1024]{1,0:T(8,128)(2,1)}, u32[]{:S(2)}, u32[]{:S(2)}) collective-permute-start(bf16[192,1024]{1,0:T(8,128)(2,1)} %get-tuple-element.87), channel_id=1, source_target_pairs={{0,1},{1,0},{2,3},{3,2},{4,5},{5,4},{6,7},{7,6},{8,9},{9,8},{10,11... | collective-permute-start | bytes 1179656 | tf_op jit(solution)/shard_map/ppermute | solution.py:346
  239.6 23.1 %collective-permute-start.30 = (bf16[192,1024]{1,0:T(8,128)(2,1)}, bf16[192,1024]{1,0:T(8,128)(2,1)}, u32[]{:S(2)}, u32[]{:S(2)}) collective-permute-start(bf16[192,1024]{1,0:T(8,128)(2,1)} %get-tuple-element.88), channel_id=1, source_target_pairs={{0,2},{1,3},{2,0},{3,1},{4,6},{5,7},{6,4},{7,5},{8,10},{9,11},{10,... | collective-permute-start | bytes 1179656 | tf_op jit(solution)/shard_map/ppermute | solution.py:346
  243.9 24.8 %collective-permute-start.31 = (bf16[192,1024]{1,0:T(8,128)(2,1)}, bf16[192,1024]{1,0:T(8,128)(2,1)}, u32[]{:S(2)}, u32[]{:S(2)}) collective-permute-start(bf16[192,1024]{1,0:T(8,128)(2,1)} %get-tuple-element.89), channel_id=1, source_target_pairs={{0,3},{1,2},{2,1},{3,0},{4,7},{5,6},{6,5},{7,4},{8,11},{9,10},{10,... | collective-permute-start | bytes 1179656 | tf_op jit(solution)/shard_map/ppermute | solution.py:346
  253.8 14.9 %collective-permute-start.32 = (bf16[64,1024]{1,0:T(8,128)(2,1)S(1)}, bf16[64,1024]{1,0:T(8,128)(2,1)S(1)}, u32[]{:S(2)}, u32[]{:S(2)}) collective-permute-start(bf16[64,1024]{1,0:T(8,128)(2,1)S(1)} %get-tuple-element.91), channel_id=1, source_target_pairs={{0,1},{1,0},{2,3},{3,2},{4,5},{5,4},{6,7},{7,6},{8,9},{9,8},{10,11... | collective-permute-start | bytes 393224 | tf_op jit(solution)/shard_map/ppermute | solution.py:346
  253.8 14.9 %collective-permute-start.33 = (bf16[64,1024]{1,0:T(8,128)(2,1)S(1)}, bf16[64,1024]{1,0:T(8,128)(2,1)S(1)}, u32[]{:S(2)}, u32[]{:S(2)}) collective-permute-start(bf16[64,1024]{1,0:T(8,128)(2,1)S(1)} %get-tuple-element.92), channel_id=1, source_target_pairs={{0,2},{1,3},{2,0},{3,1},{4,6},{5,7},{6,4},{7,5},{8,10},{9,11},{10,... | collective-permute-start | bytes 393224 | tf_op jit(solution)/shard_map/ppermute | solution.py:346
  258.1 11.8 %collective-permute-start.34 = (bf16[64,1024]{1,0:T(8,128)(2,1)S(1)}, bf16[64,1024]{1,0:T(8,128)(2,1)S(1)}, u32[]{:S(2)}, u32[]{:S(2)}) collective-permute-start(bf16[64,1024]{1,0:T(8,128)(2,1)S(1)} %get-tuple-element.93), channel_id=1, source_target_pairs={{0,3},{1,2},{2,1},{3,0},{4,7},{5,6},{6,5},{7,4},{8,11},{9,10},{10,... | collective-permute-start | bytes 393224 | tf_op jit(solution)/shard_map/ppermute | solution.py:346
  282.6 55.9 %all-to-all-start.3 = ((bf16[32,48,128]{2,1,0:T(8,128)(2,1)}), bf16[32,48,128]{2,1,0:T(8,128)(2,1)S(1)}, u32[]{:S(2)}, u32[]{:S(2)}) async-start(bf16[32,48,128]{2,1,0:T(8,128)(2,1)} %shard_map.113), calls=%async_computation.3 | async-start | bytes 786432 | tf_op jit(solution)/shard_map/all_to_all | solution.py:516
  291.0 15.1 %collective-permute-start.22 = (bf16[1024,128]{1,0:T(8,128)(2,1)}, bf16[1024,128]{1,0:T(8,128)(2,1)S(1)}, u32[]{:S(2)}, u32[]{:S(2)}) collective-permute-start(bf16[1024,128]{1,0:T(8,128)(2,1)} %copy-done.44), channel_id=1, source_target_pairs={{0,2},{1,3},{2,0},{3,1},{4,6},{5,7},{6,4},{7,5},{8,10},{9,11},{10,... | collective-permute-start | bytes 786440 | tf_op jit(solution)/shard_map/ppermute | solution.py:346
  293.6 15.8 %collective-permute-start.23 = (bf16[1024,128]{1,0:T(8,128)(2,1)}, bf16[1024,128]{1,0:T(8,128)(2,1)S(1)}, u32[]{:S(2)}, u32[]{:S(2)}) collective-permute-start(bf16[1024,128]{1,0:T(8,128)(2,1)} %copy-done.39), channel_id=1, source_target_pairs={{0,3},{1,2},{2,1},{3,0},{4,7},{5,6},{6,5},{7,4},{8,11},{9,10},{10,... | collective-permute-start | bytes 786440 | tf_op jit(solution)/shard_map/ppermute | solution.py:346
  295.7 14.4 %collective-permute-start.24 = (bf16[1024,128]{1,0:T(8,128)(2,1)}, bf16[1024,128]{1,0:T(8,128)(2,1)S(1)}, u32[]{:S(2)}, u32[]{:S(2)}) collective-permute-start(bf16[1024,128]{1,0:T(8,128)(2,1)} %copy-done.38), channel_id=1, source_target_pairs={{0,4},{1,5},{2,6},{3,7},{4,0},{5,1},{6,2},{7,3},{8,12},{9,13},{10,... | collective-permute-start | bytes 786440 | tf_op jit(solution)/shard_map/ppermute | solution.py:346
  297.5 14.7 %collective-permute-start.25 = (bf16[1024,128]{1,0:T(8,128)(2,1)}, bf16[1024,128]{1,0:T(8,128)(2,1)S(1)}, u32[]{:S(2)}, u32[]{:S(2)}) collective-permute-start(bf16[1024,128]{1,0:T(8,128)(2,1)} %copy-done.37), channel_id=1, source_target_pairs={{0,5},{1,4},{2,7},{3,6},{4,1},{5,0},{6,3},{7,2},{8,13},{9,12},{10,... | collective-permute-start | bytes 786440 | tf_op jit(solution)/shard_map/ppermute | solution.py:346
  300.4 18.4 %collective-permute-start.26 = (bf16[1024,128]{1,0:T(8,128)(2,1)}, bf16[1024,128]{1,0:T(8,128)(2,1)S(1)}, u32[]{:S(2)}, u32[]{:S(2)}) collective-permute-start(bf16[1024,128]{1,0:T(8,128)(2,1)} %copy-done.36), channel_id=1, source_target_pairs={{0,6},{1,7},{2,4},{3,5},{4,2},{5,3},{6,0},{7,1},{8,14},{9,15},{10,... | collective-permute-start | bytes 786440 | tf_op jit(solution)/shard_map/ppermute | solution.py:346
  306.1 19.0 %collective-permute-start.27 = (bf16[1024,128]{1,0:T(8,128)(2,1)}, bf16[1024,128]{1,0:T(8,128)(2,1)}, u32[]{:S(2)}, u32[]{:S(2)}) collective-permute-start(bf16[1024,128]{1,0:T(8,128)(2,1)} %copy-done.35), channel_id=1, source_target_pairs={{0,7},{1,6},{2,5},{3,4},{4,3},{5,2},{6,1},{7,0},{8,15},{9,14},{10,... | collective-permute-start | bytes 786440 | tf_op jit(solution)/shard_map/ppermute | solution.py:346
  (63 other events, 452.3 us)
where the time goes:
time: 345 us; the launch traced here: 340 us
  waiting for transfers between devices  141 us (41%)
  starting transfers between devices  96.2 us (28%)
  Pallas kernels  67.5 us (20%)
  local copies, waits for them, and re-layouts  34.3 us (10%)
    ppermute x32, waiting for transfers between devices, swap(): lax.ppermute(x, 'chan', [(i, i ^ r) for i in range(n)])  79.6 us
    ppermute x32, starting transfers between devices, swap(): lax.ppermute(x, 'chan', [(i, i ^ r) for i in range(n)])  62.5 us
    ppermute x4, waiting for transfers between devices, across(): return lax.ppermute(x, 'seq', [(i, i ^ bit) for i in range(seqs)])  43.3 us
    unnamed x112, local copies, waits for them, and re-layouts  33.7 us
    all_to_all x1, waiting for transfers between devices, local(): lax.all_to_all(inputs.reshape(n, part, width), 'chan', split_axis=0, conc...  18.3 us
    all_to_all x1, starting transfers between devices, local(): lax.all_to_all(scaled, 'seq', split_axis=0, concat_axis=0, tiled=True)  10.1 us
    all_to_all x1, starting transfers between devices, local(): got = lax.all_to_all(packed, 'seq', split_axis=0, concat_axis=0, tiled=True)  8.32 us
    pallas_call x1, Pallas kernels, local(): call(functools.partial(kernel_grad_body, heads=heads, n=n, seqs=seqs), (h...  8.19 us
  transfers between devices with their start and end apart: 40, of which 23 were waited for; matrix products, arithmetic and copies ran while one was open for 0% of the time, Pallas kernels for 16%

commit v1 on v0

--- a/solution.py
+++ b/solution.py
@@ -481,7 +481,8 @@
         cube, 2 * cube,
     )(pre, mine, across(other), lefts)
     sums = [swap(r, sums_out[r]) for r in range(ways)]
-    hs = swaps(back_out[:n])
+    hs = [swap(r, back_out[r]) for r in range(ways)]
+    hs += [swap(r, back_out[r]) for r in range(ways, n)]
 
     kernel_out = call(
         functools.partial(kernel_grad_body, heads=heads, n=n, seqs=seqs), (heads // step,),
@@ -504,6 +505,7 @@
         cube, 2 * cube,
     )(pre, *sums, *rights)
 
+    cross = swap(ways, send)
     slots = 2 * count + model_width * model_width // (n * seqs * 128)
     packed = call(
         functools.partial(pack_body, seqs=seqs, per=per), (1,),
@@ -512,7 +514,7 @@
         S((seqs, slots, 128), BF16),
         [pltpu.VMEM((seqs * slots, 128), F32)],
         cube, cube,
-    )(pre, keep, swap(ways, send))
+    )(pre, keep, cross)
     got = lax.all_to_all(packed, "seq", split_axis=0, concat_axis=0, tiled=True)
 
     input_grad = call(

time: 345 us -> 345 us (level)
  no operation moved by 1% of the time
where the time goes in v1:
time: 345 us; the launch traced here: 340 us
  waiting for transfers between devices  141 us (41%)
  starting transfers between devices  96.2 us (28%)
  Pallas kernels  67.5 us (20%)
  local copies, waits for them, and re-layouts  34.3 us (10%)
    ppermute x32, waiting for transfers between devices, swap(): lax.ppermute(x, 'chan', [(i, i ^ r) for i in range(n)])  79.6 us
    ppermute x32, starting transfers between devices, swap(): lax.ppermute(x, 'chan', [(i, i ^ r) for i in range(n)])  62.5 us
    ppermute x4, waiting for transfers between devices, across(): return lax.ppermute(x, 'seq', [(i, i ^ bit) for i in range(seqs)])  43.3 us
    unnamed x112, local copies, waits for them, and re-layouts  33.7 us
    all_to_all x1, waiting for transfers between devices, local(): lax.all_to_all(inputs.reshape(n, part, width), 'chan', split_axis=0, conc...  18.3 us
    all_to_all x1, starting transfers between devices, local(): lax.all_to_all(scaled, 'seq', split_axis=0, concat_axis=0, tiled=True)  10.1 us
    all_to_all x1, starting transfers between devices, local(): got = lax.all_to_all(packed, 'seq', split_axis=0, concat_axis=0, tiled=True)  8.32 us
    pallas_call x1, Pallas kernels, local(): call(functools.partial(kernel_grad_body, heads=heads, n=n, seqs=seqs), (h...  8.19 us
  transfers between devices with their start and end apart: 40, of which 23 were waited for; matrix products, arithmetic and copies ran while one was open for 0% of the time, Pallas kernels for 16%

profile of v1, /device:TPU:2, one launch (start us, length us, event | category | flops | bytes accessed | tf_op | source)
XLA Modules:
  0.0 340.4 jit_solution(2270396454564233074)
XLA Ops:
  0.7 6.2 %all-to-all-start.1 = ((bf16[8,1024,128]{2,1,0:T(8,128)(2,1)}), bf16[8,1024,128]{2,1,0:T(8,128)(2,1)S(1)}, u32[]{:S(2)}, u32[]{:S(2)}) async-start(bf16[8,1024,128]{2,1,0:T(8,128)(2,1)} %bitcast.20), calls=%async_computation.1 | async-start | bytes 4194304 | tf_op jit(solution)/shard_map/all_to_all | solution.py:362
  6.9 5.4 %shard_map.101 = (bf16[16,512,128]{2,1,0:T(8,128)(2,1)S(1)}, bf16[32,16,16,128]{3,2,1,0:T(8,128)(2,1)S(1)}) custom-call(s32[3]{0:T(128)S(1)} %pad_add_fusion.me, bf16[16,512,128]{2,1,0:T(8,128)(2,1)} %bitcast.21, bf16[16,512,128]{2,1,0:T(8,128)(2,1)} %k_ref.3, bf16[512,512]{1,0:T(8,128)(2,1)S(1)} %copy-done.2), custom_call_target="tpu_custom_call" | custom-call | flops 1073741824 | bytes 8388608 | tf_op jit(solution)/shard_map/pallas_call | solution.py:377
  15.0 18.3 %all-to-all-done.1.x_ref = bf16[8,1024,128]{2,1,0:T(8,128)(2,1)S(1)} async-done(((bf16[8,1024,128]{2,1,0:T(8,128)(2,1)}), bf16[8,1024,128]{2,1,0:T(8,128)(2,1)S(1)}, u32[]{:S(2)}, u32[]{:S(2)}) %all-to-all-start.1) | async-done | bytes 2097184 | tf_op jit(solution)/shard_map/all_to_all | solution.py:362
  34.6 10.1 %all-to-all-start = ((bf16[32,16,16,128]{3,2,1,0:T(8,128)(2,1)}), bf16[32,16,16,128]{3,2,1,0:T(8,128)(2,1)S(1)}, u32[]{:S(2)}, u32[]{:S(2)}) async-start(bf16[32,16,16,128]{3,2,1,0:T(8,128)(2,1)} %copy-done.6), calls=%async_computation | async-start | bytes 4194304 | tf_op jit(solution)/shard_map/all_to_all | solution.py:385
  47.4 7.2 %collective-permute-done.7 = bf16[256,128]{1,0:T(8,128)(2,1)S(1)} collective-permute-done((bf16[256,128]{1,0:T(8,128)(2,1)S(1)}, bf16[256,128]{1,0:T(8,128)(2,1)S(1)}, u32[]{:S(2)}, u32[]{:S(2)}) %collective-permute-start.7) | collective-permute-done | bytes 65568 | tf_op jit(solution)/shard_map/ppermute | solution.py:346
  64.7 38.7 %collective-permute-done.11.refs_1_ = bf16[4,2,256,128]{3,2,1,0:T(8,128)(2,1)S(1)} collective-permute-done((bf16[4,2,256,128]{3,2,1,0:T(8,128)(2,1)S(1)}, bf16[4,2,256,128]{3,2,1,0:T(8,128)(2,1)S(1)}, u32[]{:S(2)}, u32[]{:S(2)}) %collective-permute-start.11) | collective-permute-done | bytes 524320 | tf_op jit(solution)/shard_map/ppermute | solution.py:352
  105.3 6.9 %shard_map.103 = (bf16[1024,128]{1,0:T(8,128)(2,1)S(1)}, bf16[1024,128]{1,0:T(8,128)(2,1)S(1)}, bf16[1024,128]{1,0:T(8,128)(2,1)S(1)}, bf16[1024,128]{1,0:T(8,12...) custom-call(s32[3]{0:T(128)S(1)} %pad_add_fusion.me, ...), custom_call_target="tpu_custom_call" | custom-call | flops 2147483648 | bytes 8388608 | tf_op jit(solution)/shard_map/pallas_call | solution.py:389
  122.9 4.7 %collective-permute-start.19 = (bf16[1024,128]{1,0:T(8,128)(2,1)}, bf16[1024,128]{1,0:T(8,128)(2,1)}, u32[]{:S(2)}, u32[]{:S(2)}) collective-permute-start(bf16[1024,128]{1,0:T(8,128)(2,1)} %get-tuple-element.67.refs_14_), channel_id=1, source_target_pairs={{0,6},{1,7},{2,4},{3,5},{4,2},{5,3},{6,0},{7,1},{8,14},{9,15},{10,... | collective-permute-start | bytes 786440 | tf_op jit(solution)/shard_map/ppermute | solution.py:346
  127.6 3.3 collective-permute-done.15.refs_2_
  134.6 6.4 %shard_map.102 = (bf16[1024,128]{1,0:T(8,128)(2,1)S(1)}, bf16[1024,128]{1,0:T(8,128)(2,1)S(1)}, bf16[1024,128]{1,0:T(8,128)(2,1)S(1)}, bf16[1024,128]{1,0:T(8,12...) custom-call(s32[3]{0:T(128)S(1)} %pad_add_fusion.me, ...), custom_call_target="tpu_custom_call" | custom-call | flops 1073741824 | bytes 6291456 | tf_op jit(solution)/shard_map/pallas_call | solution.py:405
  147.6 8.0 %shard_map.104 = (bf16[32,16,16,128]{3,2,1,0:T(8,128)(2,1)S(1)}, bf16[8,512,256]{2,1,0:T(8,128)(2,1)}) custom-call(s32[3]{0:T(128)S(1)} %pad_add_fusion.me, bf16[1024,128]{1,0:T(8,128)(2,1)S(1)} %copy-done.17, bf16[1024,128]{1,0:T(8,128)(2,1)S(1)} %copy-done.20, bf16[1024,128]{1,0:T(8,128)(2,1)S(1)} %copy-done.22, ...), custom_call_target="tpu_custom_call" | custom-call | flops 1073741824 | bytes 8388608 | tf_op jit(solution)/shard_map/pallas_call | solution.py:415
  156.9 7.6 %all-to-all-start.2 = ((bf16[32,16,16,128]{3,2,1,0:T(8,128)(2,1)}), bf16[32,16,16,128]{3,2,1,0:T(8,128)(2,1)}, u32[]{:S(2)}, u32[]{:S(2)}) async-start(bf16[32,16,16,128]{3,2,1,0:T(8,128)(2,1)} %copy-done.7), calls=%async_computation.2 | async-start | bytes 4194304 | tf_op jit(solution)/shard_map/all_to_all | solution.py:423
  165.5 9.5 %collective-permute-start.1 = (bf16[1024,128]{1,0:T(8,128)(2,1)}, bf16[1024,128]{1,0:T(8,128)(2,1)S(1)}, u32[]{:S(2)}, u32[]{:S(2)}) collective-permute-start(bf16[1024,128]{1,0:T(8,128)(2,1)} %copy-done.53), channel_id=1, source_target_pairs={{0,2},{1,3},{2,0},{3,1},{4,6},{5,7},{6,4},{7,5},{8,10},{9,11},{10,... | collective-permute-start | bytes 786440 | tf_op jit(solution)/shard_map/ppermute | solution.py:346
  177.9 4.2 %collective-permute-start.5 = (bf16[1024,128]{1,0:T(8,128)(2,1)S(1)}, bf16[1024,128]{1,0:T(8,128)(2,1)S(1)}, u32[]{:S(2)}, u32[]{:S(2)}) collective-permute-start(bf16[1024,128]{1,0:T(8,128)(2,1)S(1)} %copy-done.49), channel_id=1, source_target_pairs={{0,6},{1,7},{2,4},{3,5},{4,2},{5,3},{6,0},{7,1},{8,14},{9,15},{10,... | collective-permute-start | bytes 786440 | tf_op jit(solution)/shard_map/ppermute | solution.py:346
  182.1 5.2 %collective-permute-done.1.refs_2_ = bf16[1024,128]{1,0:T(8,128)(2,1)S(1)} collective-permute-done((bf16[1024,128]{1,0:T(8,128)(2,1)}, bf16[1024,128]{1,0:T(8,128)(2,1)S(1)}, u32[]{:S(2)}, u32[]{:S(2)}) %collective-permute-start.1) | collective-permute-done | bytes 262176 | tf_op jit(solution)/shard_map/ppermute | solution.py:346
  188.9 4.3 %shard_map.109.xt_ref = bf16[1024,1024]{1,0:T(8,128)(2,1)S(1)} custom-call(s32[3]{0:T(128)S(1)} %pad_add_fusion.me, bf16[8,1024,128]{2,1,0:T(8,128)(2,1)S(1)} %copy-done.5), custom_call_target="tpu_custom_call" | custom-call | flops 2147483648 | bytes 4194304 | tf_op jit(solution)/shard_map/pallas_call | solution.py:439
  193.3 3.4 %shard_map.105.refs_17_.left_ref = bf16[8,32,1024]{2,1,0:T(8,128)(2,1)S(1)} custom-call(s32[3]{0:T(128)S(1)} %pad_add_fusion.me, bf16[8,512,256]{2,1,0:T(8,128)(2,1)S(1)} %copy-done.10, bf16[32,16,16,128]{3,2,1,0:T(8,128)(2,1)S(1)} %all-to-all-done.p_ref, bf16[1024,128]{1,0:T(8,128)(2,1)S(1)} %copy-done.15), custom_call_target="tpu_custom_call" | custom-call | flops 1073741824 | bytes 4194304 | tf_op jit(solution)/shard_map/pallas_call | solution.py:426
  199.8 11.2 %collective-permute-done.5.refs_6_ = bf16[1024,128]{1,0:T(8,128)(2,1)S(1)} collective-permute-done((bf16[1024,128]{1,0:T(8,128)(2,1)S(1)}, bf16[1024,128]{1,0:T(8,128)(2,1)S(1)}, u32[]{:S(2)}, u32[]{:S(2)}) %collective-permute-start.5) | collective-permute-done | bytes 262176 | tf_op jit(solution)/shard_map/ppermute | solution.py:346
  211.0 7.3 %collective-permute-done.6.refs_7_ = bf16[1024,128]{1,0:T(8,128)(2,1)S(1)} collective-permute-done((bf16[1024,128]{1,0:T(8,128)(2,1)S(1)}, bf16[1024,128]{1,0:T(8,128)(2,1)S(1)}, u32[]{:S(2)}, u32[]{:S(2)}) %collective-permute-start.6) | collective-permute-done | bytes 262176 | tf_op jit(solution)/shard_map/ppermute | solution.py:346
  218.3 6.3 %shard_map.106 = (bf16[1024,128]{1,0:T(8,128)(2,1)S(1)}, bf16[1024,128]{1,0:T(8,128)(2,1)S(1)}, bf16[1024,128]{1,0:T(8,128)(2,1)S(1)}, bf16[1024,128]{1,0:T(8,12...) custom-call(s32[3]{0:T(128)S(1)} %pad_add_fusion.me, ...), custom_call_target="tpu_custom_call" | custom-call | flops 2147483648 | bytes 10485760 | tf_op jit(solution)/shard_map/pallas_call | solution.py:448
  229.6 5.5 %shard_map.110 = (bf16[512,1024]{1,0:T(8,128)(2,1)S(1)}, bf16[512,1024]{1,0:T(8,128)(2,1)S(1)}) custom-call(s32[3]{0:T(128)S(1)} %pad_add_fusion.me, bf16[1024,1024]{1,0:T(8,128)(2,1)S(1)} %shard_map.109.xt_ref, bf16[1024,1024]{1,0:T(8,128)(2,1)} %get-tuple-element.83.gp_ref), custom_call_target="tpu_custom_call" | custom-call | flops 2147483648 | bytes 6291456 | tf_op jit(solution)/shard_map/pallas_call | solution.py:459
  239.6 4.3 %collective-permute-start.30 = (bf16[192,1024]{1,0:T(8,128)(2,1)}, bf16[192,1024]{1,0:T(8,128)(2,1)}, u32[]{:S(2)}, u32[]{:S(2)}) collective-permute-start(bf16[192,1024]{1,0:T(8,128)(2,1)} %get-tuple-element.88), channel_id=1, source_target_pairs={{0,2},{1,3},{2,0},{3,1},{4,6},{5,7},{6,4},{7,5},{8,10},{9,11},{10,... | collective-permute-start | bytes 1179656 | tf_op jit(solution)/shard_map/ppermute | solution.py:346
  244.3 8.2 %shard_map.107 = (bf16[16,512,128]{2,1,0:T(8,128)(2,1)}, bf16[16,512,128]{2,1,0:T(8,128)(2,1)S(1)}, bf16[64,1024]{1,0:T(8,128)(2,1)S(1)}, bf16[64,1024]{1,0:T(8,...) custom-call(s32[3]{0:T(128)S(1)} %pad_add_fusion.me, ...), custom_call_target="tpu_custom_call" | custom-call | flops 1073741824 | bytes 12582912 | tf_op jit(solution)/shard_map/pallas_call | solution.py:487
  253.8 4.3 %collective-permute-start.33 = (bf16[64,1024]{1,0:T(8,128)(2,1)S(1)}, bf16[64,1024]{1,0:T(8,128)(2,1)S(1)}, u32[]{:S(2)}, u32[]{:S(2)}) collective-permute-start(bf16[64,1024]{1,0:T(8,128)(2,1)S(1)} %get-tuple-element.92), channel_id=1, source_target_pairs={{0,2},{1,3},{2,0},{3,1},{4,6},{5,7},{6,4},{7,5},{8,10},{9,11},{10,... | collective-permute-start | bytes 393224 | tf_op jit(solution)/shard_map/ppermute | solution.py:346
  258.5 4.2 %collective-permute-done.30.refs_2_ = bf16[192,1024]{1,0:T(8,128)(2,1)} collective-permute-done((bf16[192,1024]{1,0:T(8,128)(2,1)}, bf16[192,1024]{1,0:T(8,128)(2,1)}, u32[]{:S(2)}, u32[]{:S(2)}) %collective-permute-start.30) | collective-permute-done | bytes 393248 | tf_op jit(solution)/shard_map/ppermute | solution.py:346
  262.6 6.0 %collective-permute-done.31.refs_3_ = bf16[192,1024]{1,0:T(8,128)(2,1)} collective-permute-done((bf16[192,1024]{1,0:T(8,128)(2,1)}, bf16[192,1024]{1,0:T(8,128)(2,1)}, u32[]{:S(2)}, u32[]{:S(2)}) %collective-permute-start.31) | collective-permute-done | bytes 393248 | tf_op jit(solution)/shard_map/ppermute | solution.py:346
  272.7 7.8 %collective-permute-done.35.got = bf16[128,1024]{1,0:T(8,128)(2,1)S(1)} collective-permute-done((bf16[128,1024]{1,0:T(8,128)(2,1)S(1)}, bf16[128,1024]{1,0:T(8,128)(2,1)S(1)}, u32[]{:S(2)}, u32[]{:S(2)}) %collective-permute-start.35) | collective-permute-done | bytes 262176 | tf_op jit(solution)/shard_map/ppermute | solution.py:346
  282.6 8.3 %all-to-all-start.3 = ((bf16[32,48,128]{2,1,0:T(8,128)(2,1)}), bf16[32,48,128]{2,1,0:T(8,128)(2,1)S(1)}, u32[]{:S(2)}, u32[]{:S(2)}) async-start(bf16[32,48,128]{2,1,0:T(8,128)(2,1)} %shard_map.113), calls=%async_computation.3 | async-start | bytes 786432 | tf_op jit(solution)/shard_map/all_to_all | solution.py:518
  300.4 3.5 %collective-permute-start.26 = (bf16[1024,128]{1,0:T(8,128)(2,1)}, bf16[1024,128]{1,0:T(8,128)(2,1)S(1)}, u32[]{:S(2)}, u32[]{:S(2)}) collective-permute-start(bf16[1024,128]{1,0:T(8,128)(2,1)} %copy-done.36), channel_id=1, source_target_pairs={{0,6},{1,7},{2,4},{3,5},{4,2},{5,3},{6,0},{7,1},{8,14},{9,15},{10,... | collective-permute-start | bytes 786440 | tf_op jit(solution)/shard_map/ppermute | solution.py:346
  312.9 5.9 %collective-permute-done.26.refs_6_ = bf16[1024,128]{1,0:T(8,128)(2,1)S(1)} collective-permute-done((bf16[1024,128]{1,0:T(8,128)(2,1)}, bf16[1024,128]{1,0:T(8,128)(2,1)S(1)}, u32[]{:S(2)}, u32[]{:S(2)}) %collective-permute-start.26) | collective-permute-done | bytes 262176 | tf_op jit(solution)/shard_map/ppermute | solution.py:346
  319.5 5.7 %collective-permute-done.27.refs_7_ = bf16[1024,128]{1,0:T(8,128)(2,1)} collective-permute-done((bf16[1024,128]{1,0:T(8,128)(2,1)}, bf16[1024,128]{1,0:T(8,128)(2,1)}, u32[]{:S(2)}, u32[]{:S(2)}) %collective-permute-start.27) | collective-permute-done | bytes 262176 | tf_op jit(solution)/shard_map/ppermute | solution.py:346
  332.4 6.0 %shard_map.108 = bf16[8192,128]{1,0:T(8,128)(2,1)} custom-call(s32[3]{0:T(128)S(1)} %pad_add_fusion.me, bf16[1024,128]{1,0:T(8,128)(2,1)S(1)} %get-tuple-element.71.refs_0_, bf16[1024,128]{1,0:T(8,128)(2,1)S(1)} %copy-done.24, bf16[1024,128]{1,0:T(8,128)(2,1)S(1)} %copy-done.26, bf16[1024,128]{1,0:T(8,128)(2,1)S(1)} %copy-done.28, ...), custom_call_target="tpu_custom_call" | custom-call | flops 1073741824 | bytes 6291456 | tf_op jit(solution)/shard_map/pallas_call | solution.py:520
  (180 shorter events, 95.4 us)
Async XLA Ops:
  0.7 32.6 %all-to-all-start.1 = ((bf16[8,1024,128]{2,1,0:T(8,128)(2,1)}), bf16[8,1024,128]{2,1,0:T(8,128)(2,1)S(1)}, u32[]{:S(2)}, u32[]{:S(2)}) async-start(bf16[8,1024,128]{2,1,0:T(8,128)(2,1)} %bitcast.20), calls=%async_computation.1 | async-start | bytes 4194304 | tf_op jit(solution)/shard_map/all_to_all | solution.py:362
  34.6 100.0 %all-to-all-start = ((bf16[32,16,16,128]{3,2,1,0:T(8,128)(2,1)}), bf16[32,16,16,128]{3,2,1,0:T(8,128)(2,1)S(1)}, u32[]{:S(2)}, u32[]{:S(2)}) async-start(bf16[32,16,16,128]{3,2,1,0:T(8,128)(2,1)} %copy-done.6), calls=%async_computation | async-start | bytes 4194304 | tf_op jit(solution)/shard_map/all_to_all | solution.py:385
  44.7 9.9 %collective-permute-start.7 = (bf16[256,128]{1,0:T(8,128)(2,1)S(1)}, bf16[256,128]{1,0:T(8,128)(2,1)S(1)}, u32[]{:S(2)}, u32[]{:S(2)}) collective-permute-start(bf16[256,128]{1,0:T(8,128)(2,1)S(1)} %constant_dynamic-slice_fusion), channel_id=1, source_target_pairs={{0,4},{1,5},{2,6},{3,7},{4,0},{5,1},{6,2},{7,3},{8,12},{9,13},{10,... | collective-permute-start | bytes 196616 | tf_op jit(solution)/shard_map/ppermute | solution.py:346
  63.2 40.2 %collective-permute-start.11 = (bf16[4,2,256,128]{3,2,1,0:T(8,128)(2,1)S(1)}, bf16[4,2,256,128]{3,2,1,0:T(8,128)(2,1)S(1)}, u32[]{:S(2)}, u32[]{:S(2)}) collective-permute-start(bf16[4,2,256,128]{3,2,1,0:T(8,128)(2,1)S(1)} %pad_maximum_fusion.refs_0_), channel_id=1, source_target_pairs={{0,16},{8,24},{16,0},{24,8},{32,48},{40,56},{48,32},{56,40},{64,80... | collective-permute-start | bytes 1572872 | tf_op jit(solution)/shard_map/ppermute | solution.py:352
  64.7 38.7 %collective-permute-start.12 = (bf16[4,2,256,128]{3,2,1,0:T(8,128)(2,1)S(1)}, bf16[4,2,256,128]{3,2,1,0:T(8,128)(2,1)S(1)}, u32[]{:S(2)}, u32[]{:S(2)}) collective-permute-start(bf16[4,2,256,128]{3,2,1,0:T(8,128)(2,1)S(1)} %pad_maximum_fusion.refs_0_), channel_id=1, source_target_pairs={{0,8},{8,0},{16,24},{24,16},{32,40},{40,32},{48,56},{56,48},{64,72... | collective-permute-start | bytes 1572872 | tf_op jit(solution)/shard_map/ppermute | solution.py:352
  115.0 15.9 %collective-permute-start.15 = (bf16[1024,128]{1,0:T(8,128)(2,1)S(1)}, bf16[1024,128]{1,0:T(8,128)(2,1)S(1)}, u32[]{:S(2)}, u32[]{:S(2)}) collective-permute-start(bf16[1024,128]{1,0:T(8,128)(2,1)S(1)} %get-tuple-element.63.refs_10_), channel_id=1, source_target_pairs={{0,2},{1,3},{2,0},{3,1},{4,6},{5,7},{6,4},{7,5},{8,10},{9,11},{10,... | collective-permute-start | bytes 786440 | tf_op jit(solution)/shard_map/ppermute | solution.py:346
  118.7 27.2 %collective-permute-start.16 = (bf16[1024,128]{1,0:T(8,128)(2,1)}, bf16[1024,128]{1,0:T(8,128)(2,1)}, u32[]{:S(2)}, u32[]{:S(2)}) collective-permute-start(bf16[1024,128]{1,0:T(8,128)(2,1)} %get-tuple-element.64.refs_11_), channel_id=1, source_target_pairs={{0,3},{1,2},{2,1},{3,0},{4,7},{5,6},{6,5},{7,4},{8,11},{9,10},{10,... | collective-permute-start | bytes 786440 | tf_op jit(solution)/shard_map/ppermute | solution.py:346
  119.0 27.0 %collective-permute-start.17 = (bf16[1024,128]{1,0:T(8,128)(2,1)}, bf16[1024,128]{1,0:T(8,128)(2,1)}, u32[]{:S(2)}, u32[]{:S(2)}) collective-permute-start(bf16[1024,128]{1,0:T(8,128)(2,1)} %get-tuple-element.65.refs_12_), channel_id=1, source_target_pairs={{0,4},{1,5},{2,6},{3,7},{4,0},{5,1},{6,2},{7,3},{8,12},{9,13},{10,... | collective-permute-start | bytes 786440 | tf_op jit(solution)/shard_map/ppermute | solution.py:346
  121.5 24.4 %collective-permute-start.18 = (bf16[1024,128]{1,0:T(8,128)(2,1)}, bf16[1024,128]{1,0:T(8,128)(2,1)}, u32[]{:S(2)}, u32[]{:S(2)}) collective-permute-start(bf16[1024,128]{1,0:T(8,128)(2,1)} %get-tuple-element.66.refs_13_), channel_id=1, source_target_pairs={{0,5},{1,4},{2,7},{3,6},{4,1},{5,0},{6,3},{7,2},{8,13},{9,12},{10,... | collective-permute-start | bytes 786440 | tf_op jit(solution)/shard_map/ppermute | solution.py:346
  122.9 23.1 %collective-permute-start.19 = (bf16[1024,128]{1,0:T(8,128)(2,1)}, bf16[1024,128]{1,0:T(8,128)(2,1)}, u32[]{:S(2)}, u32[]{:S(2)}) collective-permute-start(bf16[1024,128]{1,0:T(8,128)(2,1)} %get-tuple-element.67.refs_14_), channel_id=1, source_target_pairs={{0,6},{1,7},{2,4},{3,5},{4,2},{5,3},{6,0},{7,1},{8,14},{9,15},{10,... | collective-permute-start | bytes 786440 | tf_op jit(solution)/shard_map/ppermute | solution.py:346
  131.6 16.0 %collective-permute-start.20 = (bf16[1024,128]{1,0:T(8,128)(2,1)}, bf16[1024,128]{1,0:T(8,128)(2,1)}, u32[]{:S(2)}, u32[]{:S(2)}) collective-permute-start(bf16[1024,128]{1,0:T(8,128)(2,1)} %get-tuple-element.68.refs_15_), channel_id=1, source_target_pairs={{0,7},{1,6},{2,5},{3,4},{4,3},{5,2},{6,1},{7,0},{8,15},{9,14},{10,... | collective-permute-start | bytes 786440 | tf_op jit(solution)/shard_map/ppermute | solution.py:346
  156.9 87.3 %all-to-all-start.2 = ((bf16[32,16,16,128]{3,2,1,0:T(8,128)(2,1)}), bf16[32,16,16,128]{3,2,1,0:T(8,128)(2,1)}, u32[]{:S(2)}, u32[]{:S(2)}) async-start(bf16[32,16,16,128]{3,2,1,0:T(8,128)(2,1)} %copy-done.7), calls=%async_computation.2 | async-start | bytes 4194304 | tf_op jit(solution)/shard_map/all_to_all | solution.py:423
  164.5 13.4 %collective-permute-start = (bf16[1024,128]{1,0:T(8,128)(2,1)}, bf16[1024,128]{1,0:T(8,128)(2,1)S(1)}, u32[]{:S(2)}, u32[]{:S(2)}) collective-permute-start(bf16[1024,128]{1,0:T(8,128)(2,1)} %copy-done.54), channel_id=1, source_target_pairs={{0,1},{1,0},{2,3},{3,2},{4,5},{5,4},{6,7},{7,6},{8,9},{9,8},{10,11... | collective-permute-start | bytes 786440 | tf_op jit(solution)/shard_map/ppermute | solution.py:346
  165.5 21.9 %collective-permute-start.1 = (bf16[1024,128]{1,0:T(8,128)(2,1)}, bf16[1024,128]{1,0:T(8,128)(2,1)S(1)}, u32[]{:S(2)}, u32[]{:S(2)}) collective-permute-start(bf16[1024,128]{1,0:T(8,128)(2,1)} %copy-done.53), channel_id=1, source_target_pairs={{0,2},{1,3},{2,0},{3,1},{4,6},{5,7},{6,4},{7,5},{8,10},{9,11},{10,... | collective-permute-start | bytes 786440 | tf_op jit(solution)/shard_map/ppermute | solution.py:346
  175.0 22.6 %collective-permute-start.2 = (bf16[1024,128]{1,0:T(8,128)(2,1)}, bf16[1024,128]{1,0:T(8,128)(2,1)S(1)}, u32[]{:S(2)}, u32[]{:S(2)}) collective-permute-start(bf16[1024,128]{1,0:T(8,128)(2,1)} %copy-done.52), channel_id=1, source_target_pairs={{0,3},{1,2},{2,1},{3,0},{4,7},{5,6},{6,5},{7,4},{8,11},{9,10},{10,... | collective-permute-start | bytes 786440 | tf_op jit(solution)/shard_map/ppermute | solution.py:346
  175.0 22.6 %collective-permute-start.3 = (bf16[1024,128]{1,0:T(8,128)(2,1)}, bf16[1024,128]{1,0:T(8,128)(2,1)S(1)}, u32[]{:S(2)}, u32[]{:S(2)}) collective-permute-start(bf16[1024,128]{1,0:T(8,128)(2,1)} %copy-done.51), channel_id=1, source_target_pairs={{0,4},{1,5},{2,6},{3,7},{4,0},{5,1},{6,2},{7,3},{8,12},{9,13},{10,... | collective-permute-start | bytes 786440 | tf_op jit(solution)/shard_map/ppermute | solution.py:346
  175.6 24.3 %collective-permute-start.4 = (bf16[1024,128]{1,0:T(8,128)(2,1)}, bf16[1024,128]{1,0:T(8,128)(2,1)S(1)}, u32[]{:S(2)}, u32[]{:S(2)}) collective-permute-start(bf16[1024,128]{1,0:T(8,128)(2,1)} %copy-done.50), channel_id=1, source_target_pairs={{0,5},{1,4},{2,7},{3,6},{4,1},{5,0},{6,3},{7,2},{8,13},{9,12},{10,... | collective-permute-start | bytes 786440 | tf_op jit(solution)/shard_map/ppermute | solution.py:346
  177.9 33.1 %collective-permute-start.5 = (bf16[1024,128]{1,0:T(8,128)(2,1)S(1)}, bf16[1024,128]{1,0:T(8,128)(2,1)S(1)}, u32[]{:S(2)}, u32[]{:S(2)}) collective-permute-start(bf16[1024,128]{1,0:T(8,128)(2,1)S(1)} %copy-done.49), channel_id=1, source_target_pairs={{0,6},{1,7},{2,4},{3,5},{4,2},{5,3},{6,0},{7,1},{8,14},{9,15},{10,... | collective-permute-start | bytes 786440 | tf_op jit(solution)/shard_map/ppermute | solution.py:346
  187.3 31.0 %collective-permute-start.6 = (bf16[1024,128]{1,0:T(8,128)(2,1)S(1)}, bf16[1024,128]{1,0:T(8,128)(2,1)S(1)}, u32[]{:S(2)}, u32[]{:S(2)}) collective-permute-start(bf16[1024,128]{1,0:T(8,128)(2,1)S(1)} %copy-done.47), channel_id=1, source_target_pairs={{0,7},{1,6},{2,5},{3,4},{4,3},{5,2},{6,1},{7,0},{8,15},{9,14},{10,... | collective-permute-start | bytes 786440 | tf_op jit(solution)/shard_map/ppermute | solution.py:346
  239.5 18.5 %collective-permute-start.29 = (bf16[192,1024]{1,0:T(8,128)(2,1)}, bf16[192,1024]{1,0:T(8,128)(2,1)}, u32[]{:S(2)}, u32[]{:S(2)}) collective-permute-start(bf16[192,1024]{1,0:T(8,128)(2,1)} %get-tuple-element.87), channel_id=1, source_target_pairs={{0,1},{1,0},{2,3},{3,2},{4,5},{5,4},{6,7},{7,6},{8,9},{9,8},{10,11... | collective-permute-start | bytes 1179656 | tf_op jit(solution)/shard_map/ppermute | solution.py:346
  239.6 23.1 %collective-permute-start.30 = (bf16[192,1024]{1,0:T(8,128)(2,1)}, bf16[192,1024]{1,0:T(8,128)(2,1)}, u32[]{:S(2)}, u32[]{:S(2)}) collective-permute-start(bf16[192,1024]{1,0:T(8,128)(2,1)} %get-tuple-element.88), channel_id=1, source_target_pairs={{0,2},{1,3},{2,0},{3,1},{4,6},{5,7},{6,4},{7,5},{8,10},{9,11},{10,... | collective-permute-start | bytes 1179656 | tf_op jit(solution)/shard_map/ppermute | solution.py:346
  243.9 24.8 %collective-permute-start.31 = (bf16[192,1024]{1,0:T(8,128)(2,1)}, bf16[192,1024]{1,0:T(8,128)(2,1)}, u32[]{:S(2)}, u32[]{:S(2)}) collective-permute-start(bf16[192,1024]{1,0:T(8,128)(2,1)} %get-tuple-element.89), channel_id=1, source_target_pairs={{0,3},{1,2},{2,1},{3,0},{4,7},{5,6},{6,5},{7,4},{8,11},{9,10},{10,... | collective-permute-start | bytes 1179656 | tf_op jit(solution)/shard_map/ppermute | solution.py:346
  253.8 14.9 %collective-permute-start.32 = (bf16[64,1024]{1,0:T(8,128)(2,1)S(1)}, bf16[64,1024]{1,0:T(8,128)(2,1)S(1)}, u32[]{:S(2)}, u32[]{:S(2)}) collective-permute-start(bf16[64,1024]{1,0:T(8,128)(2,1)S(1)} %get-tuple-element.91), channel_id=1, source_target_pairs={{0,1},{1,0},{2,3},{3,2},{4,5},{5,4},{6,7},{7,6},{8,9},{9,8},{10,11... | collective-permute-start | bytes 393224 | tf_op jit(solution)/shard_map/ppermute | solution.py:346
  253.8 14.9 %collective-permute-start.33 = (bf16[64,1024]{1,0:T(8,128)(2,1)S(1)}, bf16[64,1024]{1,0:T(8,128)(2,1)S(1)}, u32[]{:S(2)}, u32[]{:S(2)}) collective-permute-start(bf16[64,1024]{1,0:T(8,128)(2,1)S(1)} %get-tuple-element.92), channel_id=1, source_target_pairs={{0,2},{1,3},{2,0},{3,1},{4,6},{5,7},{6,4},{7,5},{8,10},{9,11},{10,... | collective-permute-start | bytes 393224 | tf_op jit(solution)/shard_map/ppermute | solution.py:346
  258.1 11.8 %collective-permute-start.34 = (bf16[64,1024]{1,0:T(8,128)(2,1)S(1)}, bf16[64,1024]{1,0:T(8,128)(2,1)S(1)}, u32[]{:S(2)}, u32[]{:S(2)}) collective-permute-start(bf16[64,1024]{1,0:T(8,128)(2,1)S(1)} %get-tuple-element.93), channel_id=1, source_target_pairs={{0,3},{1,2},{2,1},{3,0},{4,7},{5,6},{6,5},{7,4},{8,11},{9,10},{10,... | collective-permute-start | bytes 393224 | tf_op jit(solution)/shard_map/ppermute | solution.py:346
  282.6 55.9 %all-to-all-start.3 = ((bf16[32,48,128]{2,1,0:T(8,128)(2,1)}), bf16[32,48,128]{2,1,0:T(8,128)(2,1)S(1)}, u32[]{:S(2)}, u32[]{:S(2)}) async-start(bf16[32,48,128]{2,1,0:T(8,128)(2,1)} %shard_map.113), calls=%async_computation.3 | async-start | bytes 786432 | tf_op jit(solution)/shard_map/all_to_all | solution.py:518
  291.0 15.1 %collective-permute-start.22 = (bf16[1024,128]{1,0:T(8,128)(2,1)}, bf16[1024,128]{1,0:T(8,128)(2,1)S(1)}, u32[]{:S(2)}, u32[]{:S(2)}) collective-permute-start(bf16[1024,128]{1,0:T(8,128)(2,1)} %copy-done.44), channel_id=1, source_target_pairs={{0,2},{1,3},{2,0},{3,1},{4,6},{5,7},{6,4},{7,5},{8,10},{9,11},{10,... | collective-permute-start | bytes 786440 | tf_op jit(solution)/shard_map/ppermute | solution.py:346
  293.6 15.8 %collective-permute-start.23 = (bf16[1024,128]{1,0:T(8,128)(2,1)}, bf16[1024,128]{1,0:T(8,128)(2,1)S(1)}, u32[]{:S(2)}, u32[]{:S(2)}) collective-permute-start(bf16[1024,128]{1,0:T(8,128)(2,1)} %copy-done.39), channel_id=1, source_target_pairs={{0,3},{1,2},{2,1},{3,0},{4,7},{5,6},{6,5},{7,4},{8,11},{9,10},{10,... | collective-permute-start | bytes 786440 | tf_op jit(solution)/shard_map/ppermute | solution.py:346
  295.7 14.4 %collective-permute-start.24 = (bf16[1024,128]{1,0:T(8,128)(2,1)}, bf16[1024,128]{1,0:T(8,128)(2,1)S(1)}, u32[]{:S(2)}, u32[]{:S(2)}) collective-permute-start(bf16[1024,128]{1,0:T(8,128)(2,1)} %copy-done.38), channel_id=1, source_target_pairs={{0,4},{1,5},{2,6},{3,7},{4,0},{5,1},{6,2},{7,3},{8,12},{9,13},{10,... | collective-permute-start | bytes 786440 | tf_op jit(solution)/shard_map/ppermute | solution.py:346
  297.5 14.7 %collective-permute-start.25 = (bf16[1024,128]{1,0:T(8,128)(2,1)}, bf16[1024,128]{1,0:T(8,128)(2,1)S(1)}, u32[]{:S(2)}, u32[]{:S(2)}) collective-permute-start(bf16[1024,128]{1,0:T(8,128)(2,1)} %copy-done.37), channel_id=1, source_target_pairs={{0,5},{1,4},{2,7},{3,6},{4,1},{5,0},{6,3},{7,2},{8,13},{9,12},{10,... | collective-permute-start | bytes 786440 | tf_op jit(solution)/shard_map/ppermute | solution.py:346
  300.4 18.4 %collective-permute-start.26 = (bf16[1024,128]{1,0:T(8,128)(2,1)}, bf16[1024,128]{1,0:T(8,128)(2,1)S(1)}, u32[]{:S(2)}, u32[]{:S(2)}) collective-permute-start(bf16[1024,128]{1,0:T(8,128)(2,1)} %copy-done.36), channel_id=1, source_target_pairs={{0,6},{1,7},{2,4},{3,5},{4,2},{5,3},{6,0},{7,1},{8,14},{9,15},{10,... | collective-permute-start | bytes 786440 | tf_op jit(solution)/shard_map/ppermute | solution.py:346
  306.1 19.0 %collective-permute-start.27 = (bf16[1024,128]{1,0:T(8,128)(2,1)}, bf16[1024,128]{1,0:T(8,128)(2,1)}, u32[]{:S(2)}, u32[]{:S(2)}) collective-permute-start(bf16[1024,128]{1,0:T(8,128)(2,1)} %copy-done.35), channel_id=1, source_target_pairs={{0,7},{1,6},{2,5},{3,4},{4,3},{5,2},{6,1},{7,0},{8,15},{9,14},{10,... | collective-permute-start | bytes 786440 | tf_op jit(solution)/shard_map/ppermute | solution.py:346
  (63 other events, 452.3 us)
